TPU v7x, 32 devices: a whole 2x2x4 slice. The times are simulated.
32 devices in a mesh: slab: 4 (over x, core), kt: 8 (over z, y).
Axes of the slice: x: 2, y: 2, z: 4, core: 2. Of those that a mesh axis runs over, the one named last changes fastest.
Arguments:
- energies: float32 [4], replicated, may hold values from -0.5 to 0.1
- onsite: float32 [8, 4, 384], P('kt', 'slab'), may hold values from -3.5 to -2.5
- hamiltonian: bfloat16 [8, 4, 2, 384, 384], P('kt', 'slab'), may hold values from -0.109375 to 0.109375
- hopping: bfloat16 [8, 4, 2, 384, 384], P('kt', 'slab'), may hold values from -0.15625 to 0.15625
- contact: bfloat16 [8, 2, 384, 384], P('kt'), may hold values from -2 to 2
- previous: bfloat16 [8, 4, 4, 2, 2, 384, 384], P('kt', None, 'slab'), may hold values from -4 to 4
- neighbours: int32 [8, 2], P('kt'), may hold values from 0 to 7, as said below
- mode_index: int32 [8, 2], P('kt'), may hold values from 0 to 3
- mode_strength: float32 [4], replicated, may hold values from 0.25 to 1
Outputs:
- retarded: bfloat16 [8, 4, 4, 2, 384, 384], P('kt', None, 'slab')
- lesser: bfloat16 [8, 4, 4, 2, 384, 384], P('kt', None, 'slab')
Inputs may be any that keep to these rules, and one draw needn't show every extreme that they name: neighbours[k, 0] is k - 1 or k - 2 and neighbours[k, 1] is k + 1 or k + 2, modulo 8.
All inputs are finite; a program needn't handle non-finite values.
Results may differ from a plain program's by a relative error of at most 0.017.
Values may be sent and summed in bfloat16 or wider, within the bound.
A program may use at most 128 MiB of HBM per device.

v0:
```python
import jax
import jax.numpy as jnp
from jax import lax
from jax.sharding import PartitionSpec as P

broaden = 0.05
fermi_level = 0.0
thermal = 0.1


def from_behind(value, axis, by):
    peers = lax.axis_size(axis)
    return lax.ppermute(value, axis, [(i, (i + by) % peers) for i in range(peers)])


def as_sent(value):
    return jax.tree.map(lambda a: a.astype(jnp.bfloat16) if a.dtype == jnp.float32 else a, value)


def combine(pieces):
    real_part = pieces[..., 0, 0, :, :] - pieces[..., 1, 1, :, :]
    imaginary_part = pieces[..., 0, 1, :, :] + pieces[..., 1, 0, :, :]
    return jnp.stack([real_part, imaginary_part], axis=-3)


def complex_mul(first_op, second_op):
    return combine(
        jnp.einsum("pij,qjk->pqik", first_op, second_op, preferred_element_type=jnp.float32)
    )


def adjoint(matrix):
    return jnp.stack([matrix[0].T, -matrix[1].T])


def slab_update(boundary, energy, levels, hamilton, coupling, phonon):
    moved_blocks = combine(
        jnp.einsum("pij,sqjk->spqik", coupling, boundary, preferred_element_type=jnp.float32)
    ).astype(jnp.bfloat16)
    self_both = combine(
        jnp.einsum(
            "spij,qjk->spqik", moved_blocks, adjoint(coupling), preferred_element_type=jnp.float32
        )
    )
    self_retarded = self_both[0]
    self_lesser = self_both[1]
    identity = jnp.eye(levels.shape[0], dtype=jnp.float32)
    system_real = (
        (energy - levels)[:, None] * identity
        - hamilton[0].astype(jnp.float32)
        - self_retarded[0]
        - phonon[0, 0]
    )
    system_imaginary = (
        broaden * identity - hamilton[1].astype(jnp.float32) - self_retarded[1] - phonon[0, 1]
    )
    diagonal_real = jnp.diagonal(system_real)
    diagonal_imaginary = jnp.diagonal(system_imaginary)
    modulus = diagonal_real * diagonal_real + diagonal_imaginary * diagonal_imaginary
    inverse_real = diagonal_real / modulus
    inverse_imaginary = -diagonal_imaginary / modulus
    scaled_real = (
        inverse_real[:, None] * system_real - inverse_imaginary[:, None] * system_imaginary
    )
    scaled_imaginary = (
        inverse_real[:, None] * system_imaginary + inverse_imaginary[:, None] * system_real
    )
    sandwich_real = (
        scaled_real * inverse_real[None, :] - scaled_imaginary * inverse_imaginary[None, :]
    )
    sandwich_imaginary = (
        scaled_real * inverse_imaginary[None, :] + scaled_imaginary * inverse_real[None, :]
    )
    first_guess = jnp.stack(
        [
            2.0 * jnp.diag(inverse_real) - sandwich_real,
            2.0 * jnp.diag(inverse_imaginary) - sandwich_imaginary,
        ]
    )
    first_rounded = first_guess.astype(jnp.bfloat16)
    system_rounded = jnp.stack([system_real, system_imaginary]).astype(jnp.bfloat16)
    product = complex_mul(system_rounded, first_rounded).astype(jnp.bfloat16)
    retarded = (2.0 * first_guess - complex_mul(first_rounded, product)).astype(jnp.bfloat16)
    source = (phonon[1] + self_lesser).astype(jnp.bfloat16)
    halfway = complex_mul(retarded, source).astype(jnp.bfloat16)
    lesser = complex_mul(halfway, adjoint(retarded)).astype(jnp.bfloat16)
    return (retarded, lesser)


def sweep_energy(boundary, energy, phonon, level_all, hamilton_all, coupling_all):
    slab_count = level_all.shape[0]
    retarded_list = [None] * slab_count
    lesser_list = [None] * slab_count
    for slab_num in reversed(range(slab_count)):
        ret_block, les_block = slab_update(
            boundary,
            energy,
            level_all[slab_num],
            hamilton_all[slab_num],
            coupling_all[slab_num],
            phonon[slab_num],
        )
        retarded_list[slab_num] = ret_block
        lesser_list[slab_num] = les_block
        boundary = jnp.stack([ret_block, les_block])
    return (jnp.stack(retarded_list), jnp.stack(lesser_list), boundary)


def cycle_phonon(blocks, neighbours, mode_index, mode_strength):
    nearest = [from_behind(blocks, "kt", offset) for offset in (1, -1)]
    farther = [from_behind(blocks, "kt", offset) for offset in (2, -2)]
    kpoint = lax.axis_index("kt")
    cycle_size = lax.axis_size("kt")
    neighbour_pair = neighbours[0]
    behind = jnp.where(neighbour_pair[0] == (kpoint - 1) % cycle_size, nearest[0], farther[0])
    forward = jnp.where(neighbour_pair[1] == (kpoint + 1) % cycle_size, nearest[1], farther[1])
    mode_table = jnp.arange(mode_strength.shape[0], dtype=jnp.int32)
    strength = jnp.sum(
        jnp.where(mode_index[0][:, None] == mode_table[None, :], mode_strength[None, :], 0.0),
        axis=1,
    )
    return strength[0] * behind[0].astype(jnp.float32) + strength[1] * forward[0].astype(
        jnp.float32
    )


def starting_blocks(contact, energy_list):
    contact_block = contact[0]
    contact_float = contact_block.astype(jnp.float32)
    skew_part = jnp.stack(
        [contact_float[0] - contact_float[0].T, contact_float[1] + contact_float[1].T]
    )
    occupation = 1.0 / (1.0 + jnp.exp((energy_list - fermi_level) / thermal))
    energy_count = energy_list.shape[0]
    contact_lesser = (-occupation[:, None, None, None] * skew_part).astype(jnp.bfloat16)
    return jnp.stack(
        [jnp.broadcast_to(contact_block, (energy_count,) + contact_block.shape), contact_lesser],
        axis=1,
    )


def body(
    energies, onsite, hamiltonian, hopping, contact, previous, neighbours, mode_index, mode_strength
):
    position = lax.axis_index("slab")
    regrouped = lax.all_to_all(previous, "slab", split_axis=1, concat_axis=2, tiled=True)
    phonon_all = cycle_phonon(regrouped, neighbours, mode_index, mode_strength)
    level_whole = lax.all_gather(onsite, "slab", axis=1, tiled=True)
    hamilton_whole, coupling_whole = (
        lax.all_gather(hamiltonian, "slab", axis=1, tiled=True),
        lax.all_gather(hopping, "slab", axis=1, tiled=True),
    )
    local_count = regrouped.shape[1]
    local_energies = lax.dynamic_slice_in_dim(energies, position * local_count, local_count, 0)
    initial = starting_blocks(contact, local_energies)

    def run_whole(boundary, energy, phonon):
        return sweep_energy(
            boundary, energy, phonon, level_whole[0], hamilton_whole[0], coupling_whole[0]
        )

    retarded_local, lesser_local, unused = jax.vmap(run_whole)(initial, local_energies, phonon_all)
    retarded_all, lesser_all = (
        lax.all_to_all(
            as_sent(retarded_local[None]), "slab", split_axis=2, concat_axis=1, tiled=True
        ),
        lax.all_to_all(
            as_sent(lesser_local[None]), "slab", split_axis=2, concat_axis=1, tiled=True
        ),
    )
    return (retarded_all, lesser_all)


def solution(mesh):
    in_specs = (
        P(),
        P("kt", "slab", None),
        P("kt", "slab", None, None, None),
        P("kt", "slab", None, None, None),
        P("kt", None, None, None),
        P("kt", None, "slab", None, None, None, None),
        P("kt", None),
        P("kt", None),
        P(),
    )
    out_specs = (P("kt", None, "slab", None, None, None), P("kt", None, "slab", None, None, None))
    return jax.shard_map(body, mesh=mesh, in_specs=in_specs, out_specs=out_specs, check_vma=False)
```

profile of v0, /device:TPU:0, one launch (start us, length us, event | category | flops | bytes accessed | tf_op | source)
XLA Modules:
  0.0 600.2 jit_solution(12964308768972763994)
XLA Ops:
  7.9 6.7 %copy.286 = bf16[1,4,1,2,2,384,384]{5,6,4,3,2,0,1:T(8,128)(2,1)} copy(bf16[1,4,1,2,2,384,384]{6,5,4,3,2,1,0:T(8,128)(2,1)} %param.14) | data formatting | bytes 9437184 | tf_op args[5]
  14.6 5.1 all-to-all-start
  20.4 77.7 %all-to-all-done = bf16[1,4,1,2,2,384,384]{5,6,4,3,2,0,1:T(8,128)(2,1)} async-done(((bf16[1,4,1,2,2,384,384]{5,6,4,3,2,0,1:T(8,128)(2,1)}), bf16[1,4,1,2,2,384,384]{5,6,4,3,2,0,1:T(8,128)(2,1)}, u32[]{:S(2)}, u32[]{:S(2)}) %all-to-all-start) | async-done | bytes 4718624 | tf_op jit(solution)/shard_map/all_to_all | solution.py:146
  101.1 3.2 collective-permute-start.2
  111.6 5.2 all_gather.9
  137.2 68.8 %collective-permute-done = bf16[1,1,4,2,2,384,384]{5,6,4,3,2,1,0:T(8,128)(2,1)} collective-permute-done((bf16[1,1,4,2,2,384,384]{5,6,4,3,2,1,0:T(8,128)(2,1)}, bf16[1,1,4,2,2,384,384]{5,6,4,3,2,1,0:T(8,128)(2,1)}, u32[]{:S(2)}, u32[]{:S(2)}) %collective-permute-start) | collective-permute-done | bytes 4718624 | tf_op jit(solution)/shard_map/ppermute | solution.py:13
  206.4 99.2 %collective-permute-done.2 = bf16[1,1,4,2,2,384,384]{5,6,4,3,2,1,0:T(8,128)(2,1)} collective-permute-done((bf16[1,1,4,2,2,384,384]{5,6,4,3,2,1,0:T(8,128)(2,1)}, bf16[1,1,4,2,2,384,384]{5,6,4,3,2,1,0:T(8,128)(2,1)}, u32[]{:S(2)}, u32[]{:S(2)}) %collective-permute-start.2) | collective-permute-done | bytes 4718624 | tf_op jit(solution)/shard_map/ppermute | solution.py:13
  305.6 101.7 %collective-permute-done.3 = bf16[1,1,4,2,2,384,384]{5,6,4,3,2,1,0:T(8,128)(2,1)} collective-permute-done((bf16[1,1,4,2,2,384,384]{5,6,4,3,2,1,0:T(8,128)(2,1)}, bf16[1,1,4,2,2,384,384]{5,6,4,3,2,1,0:T(8,128)(2,1)}, u32[]{:S(2)}, u32[]{:S(2)}) %collective-permute-start.3) | collective-permute-done | bytes 4718624 | tf_op jit(solution)/shard_map/ppermute | solution.py:13
  407.3 12.0 %add_bitcast_fusion = f32[1,4,2,2,384,384]{4,5,3,2,1,0:T(8,128)} fusion(bf16[1,1,4,2,2,384,384]{5,6,4,3,2,1,0:T(8,128)(2,1)} %collective-permute-done.2, bf16[1,1,4,2,2,384,384]{5,6,4,3,2,1,0:T(8,128)(2,1)} %collective-permute-done.3, f32[]{:T(128)} %bitcast.80, bf16[1,1,4,2,2,384,384]{5,6,4,3,2,1,0:T(8,128)(2,1)} %collective-permute-done, ...), kind=kLoop, calls=%fused_computation.8 | loop fusion | flops 16515072 | bytes 28311562 | tf_op jit(solution)/shard_map/add | solution.py:122
  419.3 6.6 %slice_bitcast_fusion = (f32[1,2,2,384,384]{3,4,2,1,0:T(8,128)S(1)}, f32[1,2,2,384,384]{3,4,2,1,0:T(8,128)}, f32[1,2,2,384,384]{3,4,2,1,0:T(8,128)}, f32[1,1,2,2,384,384]{4,5,3,2,1,0:T(8,128)S(1)}) fusion(f32[1,4,2,2,384,384]{4,5,3,2,1,0:T(8,128)} %add_bitcast_fusion), kind=kLoop, calls=%fused_computation.9 | loop fusion | bytes 18874368 | tf_op jit(solution)/shard_map/vmap()/squeeze | solution.py:101
  429.8 4.8 gather_fusion
  434.6 4.5 gather_fusion.1
  457.4 3.5 gather_fusion.3
  460.8 4.7 gather_fusion.2
  483.8 3.5 gather_fusion.5
  487.3 3.7 gather_fusion.4
  507.6 3.5 gather_fusion.7
  511.1 3.5 gather_fusion.6
  525.0 4.6 all-to-all-start.2
  532.9 25.3 %all-to-all-done.2 = bf16[1,1,4,2,384,384]{4,5,3,1,0,2:T(8,128)(2,1)} async-done(((bf16[1,1,4,2,384,384]{4,5,3,1,0,2:T(8,128)(2,1)}), bf16[1,1,4,2,384,384]{4,5,3,1,0,2:T(8,128)(2,1)}, u32[]{:S(2)}, u32[]{:S(2)}) %all-to-all-start.2) | async-done | bytes 2359328 | tf_op jit(solution)/shard_map/all_to_all | solution.py:167
  558.2 3.6 all-to-all-start.1
  561.9 4.3 copy.358
  566.1 24.2 %all-to-all-done.1 = bf16[1,1,4,2,384,384]{4,5,3,1,0,2:T(8,128)(2,1)S(1)} async-done(((bf16[1,1,4,2,384,384]{4,5,3,1,0,2:T(8,128)(2,1)}), bf16[1,1,4,2,384,384]{4,5,3,1,0,2:T(8,128)(2,1)S(1)}, u32[]{:S(2)}, u32[]{:S(2)}) %all-to-all-start.1) | async-done | bytes 2359328 | tf_op jit(solution)/shard_map/all_to_all | solution.py:164
  590.3 2.6 copy.357
  (287 shorter events, 100.0 us)
Async XLA Ops:
  7.2 111.8 %all-gather.3.cloned.1.call-start = ((), (), s32[]{:S(2)}) async-start(), calls=%async_computation.3 | async-start | bytes 2949120 | tf_op jit(solution)/shard_map/all_gather | solution.py:150
  14.6 90.3 %copy-start.54 = (bf16[1,2,384,384]{3,2,1,0:T(8,128)(2,1)S(1)}, bf16[1,2,384,384]{3,2,1,0:T(8,128)(2,1)}, u32[]{:S(2)}) copy-start(bf16[1,2,384,384]{3,2,1,0:T(8,128)(2,1)} %param.13) | copy-start | bytes 1769476
  14.6 83.5 %all-to-all-start = ((bf16[1,4,1,2,2,384,384]{5,6,4,3,2,0,1:T(8,128)(2,1)}), bf16[1,4,1,2,2,384,384]{5,6,4,3,2,0,1:T(8,128)(2,1)}, u32[]{:S(2)}, u32[]{:S(2)}) async-start(bf16[1,4,1,2,2,384,384]{5,6,4,3,2,0,1:T(8,128)(2,1)} %copy.286), calls=%async_computation | async-start | bytes 9437184 | tf_op jit(solution)/shard_map/all_to_all | solution.py:146
  19.6 108.4 %all-gather.5.cloned.1.call-start = ((), (), s32[]{:S(2)}) async-start(), calls=%async_computation.4 | async-start | bytes 2949120 | tf_op jit(solution)/shard_map/all_gather | solution.py:151
  98.1 107.9 %collective-permute-start = (bf16[1,1,4,2,2,384,384]{5,6,4,3,2,1,0:T(8,128)(2,1)}, bf16[1,1,4,2,2,384,384]{5,6,4,3,2,1,0:T(8,128)(2,1)}, u32[]{:S(2)}, u32[]{:S(2)}) collective-permute-start(bf16[1,1,4,2,2,384,384]{5,6,4,3,2,1,0:T(8,128)(2,1)} %bitcast.79), channel_id=1, source_target_pairs={{0,1},{1,2},{2,3},{3,4},{4,5},{5,6},{6,7},{7,0},{8,9},{9,10},{10,1... | collective-permute-start | bytes 14155784 | tf_op jit(solution)/shard_map/ppermute | solution.py:13
  99.6 106.8 %collective-permute-start.1 = (bf16[1,1,4,2,2,384,384]{5,6,4,3,2,1,0:T(8,128)(2,1)}, bf16[1,1,4,2,2,384,384]{5,6,4,3,2,1,0:T(8,128)(2,1)}, u32[]{:S(2)}, u32[]{:S(2)}) collective-permute-start(bf16[1,1,4,2,2,384,384]{5,6,4,3,2,1,0:T(8,128)(2,1)} %bitcast.79), channel_id=1, source_target_pairs={{0,2},{1,3},{2,4},{3,5},{4,6},{5,7},{6,0},{7,1},{8,10},{9,11},{10,... | collective-permute-start | bytes 14155784 | tf_op jit(solution)/shard_map/ppermute | solution.py:13
  101.1 204.6 %collective-permute-start.2 = (bf16[1,1,4,2,2,384,384]{5,6,4,3,2,1,0:T(8,128)(2,1)}, bf16[1,1,4,2,2,384,384]{5,6,4,3,2,1,0:T(8,128)(2,1)}, u32[]{:S(2)}, u32[]{:S(2)}) collective-permute-start(bf16[1,1,4,2,2,384,384]{5,6,4,3,2,1,0:T(8,128)(2,1)} %bitcast.79), channel_id=1, source_target_pairs={{0,7},{1,0},{2,1},{3,2},{4,3},{5,4},{6,5},{7,6},{8,15},{9,8},{10,9... | collective-permute-start | bytes 14155784 | tf_op jit(solution)/shard_map/ppermute | solution.py:13
  104.3 303.0 %collective-permute-start.3 = (bf16[1,1,4,2,2,384,384]{5,6,4,3,2,1,0:T(8,128)(2,1)}, bf16[1,1,4,2,2,384,384]{5,6,4,3,2,1,0:T(8,128)(2,1)}, u32[]{:S(2)}, u32[]{:S(2)}) collective-permute-start(bf16[1,1,4,2,2,384,384]{5,6,4,3,2,1,0:T(8,128)(2,1)} %bitcast.79), channel_id=1, source_target_pairs={{0,6},{1,7},{2,0},{3,1},{4,2},{5,3},{6,4},{7,5},{8,14},{9,15},{10,... | collective-permute-start | bytes 14155784 | tf_op jit(solution)/shard_map/ppermute | solution.py:13
  108.0 3.5 copy-start.74
  108.1 8.7 %copy-start.76 = (f32[4]{0:T(128)S(1)}, f32[4]{0:T(128)}, u32[]{:S(2)}) copy-start(f32[4]{0:T(128)} %param.17) | copy-start | bytes 52
  108.1 8.7 %copy-start.77 = (s32[1,2]{1,0:T(1,128)S(1)}, s32[1,2]{1,0:T(1,128)}, u32[]{:S(2)}) copy-start(s32[1,2]{1,0:T(1,128)} %param.16) | copy-start | bytes 28
  137.2 288.9 %copy-start.22 = (f32[1,2,384,384]{2,3,1,0:T(8,128)}, f32[1,2,384,384]{2,3,1,0:T(8,128)S(1)}, u32[]{:S(2)}) copy-start(f32[1,2,384,384]{2,3,1,0:T(8,128)S(1)} %fusion.7) | copy-start | bytes 3538948
  434.6 5.2 copy-start.55
  447.2 3.1 copy-start.28
  460.8 5.3 copy-start.56
  473.7 3.2 copy-start.30
  487.3 3.8 copy-start.57
  498.5 3.2 copy-start.32
  518.1 2.9 copy-start.24
  518.1 2.9 copy-start.26
  525.0 4.7 copy-start.25
  525.0 4.7 copy-start.27
  525.0 33.2 %all-to-all-start.2 = ((bf16[1,1,4,2,384,384]{4,5,3,1,0,2:T(8,128)(2,1)}), bf16[1,1,4,2,384,384]{4,5,3,1,0,2:T(8,128)(2,1)}, u32[]{:S(2)}, u32[]{:S(2)}) async-start(bf16[1,1,4,2,384,384]{4,5,3,1,0,2:T(8,128)(2,1)} %maximum_bitcast_fusion.1), calls=%async_computation.2 | async-start | bytes 4718592 | tf_op jit(solution)/shard_map/all_to_all | solution.py:167
  558.2 32.1 %all-to-all-start.1 = ((bf16[1,1,4,2,384,384]{4,5,3,1,0,2:T(8,128)(2,1)}), bf16[1,1,4,2,384,384]{4,5,3,1,0,2:T(8,128)(2,1)S(1)}, u32[]{:S(2)}, u32[]{:S(2)}) async-start(bf16[1,1,4,2,384,384]{4,5,3,1,0,2:T(8,128)(2,1)} %maximum_bitcast_fusion), calls=%async_computation.1 | async-start | bytes 4718592 | tf_op jit(solution)/shard_map/all_to_all | solution.py:164
  (63 other events, 89.1 us)
Sparse Core Ops, SparseCore 0:
  9.5 38.0 all-gather.2
  49.2 35.9 all-gather.4
where the time goes:
time: 610 us; the launch traced here: 600 us
  waiting for transfers between devices  399 us (65%)
  local copies, waits for them, and re-layouts  91.6 us (15%)
  other arithmetic  38.7 us (6%)
  matrix products  28 us (5%)
  starting transfers between devices  20.2 us (3%)
  between operations  17.8 us (3%)
    ppermute x4, waiting for transfers between devices, from_behind(): lax.ppermute(value, axis, [(i, (i + by) % peers) for i in range(peers)])  270 us
    all_to_all x1, waiting for transfers between devices, body(): lax.all_to_all(previous, 'slab', split_axis=1, concat_axis=2, tiled=True)  77.7 us
    unnamed x168, local copies, waits for them, and re-layouts  47 us
    all_to_all x1, waiting for transfers between devices, body(): lax.all_to_all(as_sent(lesser_local[None]), 'slab', split_axis=2, concat_...  25.3 us
    all_to_all x1, waiting for transfers between devices, body(): lax.all_to_all(as_sent(retarded_local[None]), 'slab', split_axis=2, conca...  24.2 us
    gather x4, local copies, waits for them, and re-layouts, slab_update(): diagonal_real = jnp.diagonal(system_real)  16.7 us
    gather x4, local copies, waits for them, and re-layouts, slab_update(): diagonal_imaginary = jnp.diagonal(system_imaginary)  14.9 us
    dot_general x16, matrix products, complex_mul(): jnp.einsum('pij,qjk->pqik', first_op, second_op, preferred_element_type=j...  12.6 us
  transfers between devices with their start and end apart: 9, of which 7 were waited for; matrix products, arithmetic and copies ran while one was open for 6% of the time, Pallas kernels for 0%

commit v1 on v0

--- a/solution.py
+++ b/solution.py
@@ -33,29 +33,38 @@
     return jnp.stack([matrix[0].T, -matrix[1].T])
 
 
+def mul_adjoint(first_op, second_op):
+    pieces = jnp.einsum("...pij,qkj->...pqik", first_op, second_op, preferred_element_type=jnp.float32)
+    real_part = pieces[..., 0, 0, :, :] + pieces[..., 1, 1, :, :]
+    imaginary_part = pieces[..., 1, 0, :, :] - pieces[..., 0, 1, :, :]
+    return jnp.stack([real_part, imaginary_part], axis=-3)
+
+
 def slab_update(boundary, energy, levels, hamilton, coupling, phonon):
     moved_blocks = combine(
         jnp.einsum("pij,sqjk->spqik", coupling, boundary, preferred_element_type=jnp.float32)
     ).astype(jnp.bfloat16)
-    self_both = combine(
-        jnp.einsum(
-            "spij,qjk->spqik", moved_blocks, adjoint(coupling), preferred_element_type=jnp.float32
-        )
-    )
+    self_both = mul_adjoint(moved_blocks, coupling)
     self_retarded = self_both[0]
     self_lesser = self_both[1]
-    identity = jnp.eye(levels.shape[0], dtype=jnp.float32)
+    size = levels.shape[0]
+    on_diagonal = lax.broadcasted_iota(jnp.int32, (size, size), 0) == lax.broadcasted_iota(
+        jnp.int32, (size, size), 1
+    )
     system_real = (
-        (energy - levels)[:, None] * identity
+        jnp.where(on_diagonal, (energy - levels)[:, None], 0.0)
         - hamilton[0].astype(jnp.float32)
         - self_retarded[0]
         - phonon[0, 0]
     )
     system_imaginary = (
-        broaden * identity - hamilton[1].astype(jnp.float32) - self_retarded[1] - phonon[0, 1]
+        jnp.where(on_diagonal, broaden, 0.0)
+        - hamilton[1].astype(jnp.float32)
+        - self_retarded[1]
+        - phonon[0, 1]
     )
-    diagonal_real = jnp.diagonal(system_real)
-    diagonal_imaginary = jnp.diagonal(system_imaginary)
+    diagonal_real = jnp.sum(jnp.where(on_diagonal, system_real, 0.0), axis=1)
+    diagonal_imaginary = jnp.sum(jnp.where(on_diagonal, system_imaginary, 0.0), axis=1)
     modulus = diagonal_real * diagonal_real + diagonal_imaginary * diagonal_imaginary
     inverse_real = diagonal_real / modulus
     inverse_imaginary = -diagonal_imaginary / modulus
@@ -73,8 +82,8 @@
     )
     first_guess = jnp.stack(
         [
-            2.0 * jnp.diag(inverse_real) - sandwich_real,
-            2.0 * jnp.diag(inverse_imaginary) - sandwich_imaginary,
+            jnp.where(on_diagonal, 2.0 * inverse_real[:, None], 0.0) - sandwich_real,
+            jnp.where(on_diagonal, 2.0 * inverse_imaginary[:, None], 0.0) - sandwich_imaginary,
         ]
     )
     first_rounded = first_guess.astype(jnp.bfloat16)
@@ -83,7 +92,7 @@
     retarded = (2.0 * first_guess - complex_mul(first_rounded, product)).astype(jnp.bfloat16)
     source = (phonon[1] + self_lesser).astype(jnp.bfloat16)
     halfway = complex_mul(retarded, source).astype(jnp.bfloat16)
-    lesser = complex_mul(halfway, adjoint(retarded)).astype(jnp.bfloat16)
+    lesser = mul_adjoint(halfway, retarded).astype(jnp.bfloat16)
     return (retarded, lesser)
 
 

time: 610 us -> 542 us (0.89); the launches traced: 600 us -> 539 us
  local copies, waits for them, and re-layouts: 91.6 us -> 38.3 us
  other arithmetic: 38.7 us -> 28.2 us
    gather x8 -> x0, local copies, waits for them, and re-layouts: 31.6 us -> none  [the longest x4 16.7 us: slab_update(): diagonal_real = jnp.diagonal(system_real)]
    unnamed x168 -> x50, local copies, waits for them, and re-layouts: 47 us -> 27.4 us
    sub x8 -> x4, other arithmetic: 8.1 us -> 0.82 us  [mul_adjoint(): imaginary_part = pieces[..., 1, 0, :, :] - pieces[..., 0, 1, :, :]]
    dot_general x16 -> x12, matrix products: 12.6 us -> 9.76 us  [complex_mul(): jnp.einsum('pij,qjk->pqik', first_op, second_op, preferred_element_type=j...]
where the time goes in v1:
time: 542 us; the launch traced here: 539 us
  waiting for transfers between devices  404 us (75%)
  local copies, waits for them, and re-layouts  38.3 us (7%)
  other arithmetic  28.2 us (5%)
  matrix products  26.4 us (5%)
  starting transfers between devices  20 us (4%)
  between operations  17 us (3%)
    ppermute x4, waiting for transfers between devices, from_behind(): lax.ppermute(value, axis, [(i, (i + by) % peers) for i in range(peers)])  274 us
    all_to_all x1, waiting for transfers between devices, body(): lax.all_to_all(previous, 'slab', split_axis=1, concat_axis=2, tiled=True)  77.7 us
    unnamed x50, local copies, waits for them, and re-layouts  27.4 us
    all_to_all x1, waiting for transfers between devices, body(): lax.all_to_all(as_sent(retarded_local[None]), 'slab', split_axis=2, conca...  25.9 us
    all_to_all x1, waiting for transfers between devices, body(): lax.all_to_all(as_sent(lesser_local[None]), 'slab', split_axis=2, concat_...  24.9 us
    add x1, other arithmetic, cycle_phonon(): strength[0] * behind[0].astype(jnp.float32)  11.8 us
  transfers between devices with their start and end apart: 9, of which 7 were waited for; matrix products, arithmetic and copies ran while one was open for 6% of the time, Pallas kernels for 0%

profile of v1, /device:TPU:0, one launch (start us, length us, event | category | flops | bytes accessed | tf_op | source)
XLA Modules:
  0.0 539.3 jit_solution(13014155300947391185)
XLA Ops:
  7.9 6.7 %copy.195 = bf16[1,4,1,2,2,384,384]{5,6,4,3,2,0,1:T(8,128)(2,1)} copy(bf16[1,4,1,2,2,384,384]{6,5,4,3,2,1,0:T(8,128)(2,1)} %param.14) | data formatting | bytes 9437184 | tf_op args[5]
  14.6 5.1 all-to-all-start
  20.4 77.7 %all-to-all-done = bf16[1,4,1,2,2,384,384]{5,6,4,3,2,0,1:T(8,128)(2,1)} async-done(((bf16[1,4,1,2,2,384,384]{5,6,4,3,2,0,1:T(8,128)(2,1)}), bf16[1,4,1,2,2,384,384]{5,6,4,3,2,0,1:T(8,128)(2,1)}, u32[]{:S(2)}, u32[]{:S(2)}) %all-to-all-start) | async-done | bytes 4718624 | tf_op jit(solution)/shard_map/all_to_all | solution.py:155
  98.1 1.5 collective-permute-start
  99.6 1.5 collective-permute-start.1
  101.1 3.2 collective-permute-start.2
  111.6 5.4 all_gather.9
  118.6 1.9 fusion.317
  127.6 2.5 convolution_bitcast_fusion.7
  130.4 2.5 convolution_bitcast_fusion.6
  133.2 72.8 %collective-permute-done = bf16[1,1,4,2,2,384,384]{5,6,4,3,2,1,0:T(8,128)(2,1)} collective-permute-done((bf16[1,1,4,2,2,384,384]{5,6,4,3,2,1,0:T(8,128)(2,1)}, bf16[1,1,4,2,2,384,384]{5,6,4,3,2,1,0:T(8,128)(2,1)}, u32[]{:S(2)}, u32[]{:S(2)}) %collective-permute-start) | collective-permute-done | bytes 4718624 | tf_op jit(solution)/shard_map/ppermute | solution.py:13
  206.4 99.2 %collective-permute-done.2 = bf16[1,1,4,2,2,384,384]{5,6,4,3,2,1,0:T(8,128)(2,1)} collective-permute-done((bf16[1,1,4,2,2,384,384]{5,6,4,3,2,1,0:T(8,128)(2,1)}, bf16[1,1,4,2,2,384,384]{5,6,4,3,2,1,0:T(8,128)(2,1)}, u32[]{:S(2)}, u32[]{:S(2)}) %collective-permute-start.2) | collective-permute-done | bytes 4718624 | tf_op jit(solution)/shard_map/ppermute | solution.py:13
  305.6 101.7 %collective-permute-done.3 = bf16[1,1,4,2,2,384,384]{5,6,4,3,2,1,0:T(8,128)(2,1)} collective-permute-done((bf16[1,1,4,2,2,384,384]{5,6,4,3,2,1,0:T(8,128)(2,1)}, bf16[1,1,4,2,2,384,384]{5,6,4,3,2,1,0:T(8,128)(2,1)}, u32[]{:S(2)}, u32[]{:S(2)}) %collective-permute-start.3) | collective-permute-done | bytes 4718624 | tf_op jit(solution)/shard_map/ppermute | solution.py:13
  407.3 11.8 %add_bitcast_fusion = f32[1,4,2,2,384,384]{4,5,3,2,1,0:T(8,128)} fusion(bf16[1,1,4,2,2,384,384]{5,6,4,3,2,1,0:T(8,128)(2,1)} %collective-permute-done.2, bf16[1,1,4,2,2,384,384]{5,6,4,3,2,1,0:T(8,128)(2,1)} %collective-permute-done.3, f32[]{:T(128)} %bitcast.42, bf16[1,1,4,2,2,384,384]{5,6,4,3,2,1,0:T(8,128)(2,1)} %collective-permute-done, ...), kind=kLoop, calls=%fused_computation | loop fusion | flops 16515072 | bytes 28311562 | tf_op jit(solution)/shard_map/add | solution.py:131
  419.1 4.4 slice_bitcast_fusion
  461.2 1.6 maximum_bitcast_fusion.1
  462.9 3.6 all-to-all-start.2
  466.5 1.8 fusion.68
  468.3 1.8 maximum_bitcast_fusion
  470.1 24.9 %all-to-all-done.2 = bf16[1,1,4,2,384,384]{4,5,3,1,0,2:T(8,128)(2,1)S(1)} async-done(((bf16[1,1,4,2,384,384]{4,5,3,1,0,2:T(8,128)(2,1)}), bf16[1,1,4,2,384,384]{4,5,3,1,0,2:T(8,128)(2,1)S(1)}, u32[]{:S(2)}, u32[]{:S(2)}) %all-to-all-start.2) | async-done | bytes 2359328 | tf_op jit(solution)/shard_map/all_to_all | solution.py:176
  494.9 4.5 all-to-all-start.1
  499.5 2.6 copy.264
  502.1 25.9 %all-to-all-done.1 = bf16[1,1,4,2,384,384]{4,5,3,1,0,2:T(8,128)(2,1)} async-done(((bf16[1,1,4,2,384,384]{4,5,3,1,0,2:T(8,128)(2,1)}), bf16[1,1,4,2,384,384]{4,5,3,1,0,2:T(8,128)(2,1)}, u32[]{:S(2)}, u32[]{:S(2)}) %all-to-all-start.1) | async-done | bytes 2359328 | tf_op jit(solution)/shard_map/all_to_all | solution.py:173
  528.0 4.3 copy.263
  (155 shorter events, 53.6 us)
Async XLA Ops:
  7.2 111.4 %all-gather.3.cloned.1.call-start = ((), (), s32[]{:S(2)}) async-start(), calls=%async_computation.3 | async-start | bytes 2949120 | tf_op jit(solution)/shard_map/all_gather | solution.py:159
  14.6 90.3 %copy-start.13 = (bf16[1,2,384,384]{3,2,1,0:T(8,128)(2,1)S(1)}, bf16[1,2,384,384]{3,2,1,0:T(8,128)(2,1)}, u32[]{:S(2)}) copy-start(bf16[1,2,384,384]{3,2,1,0:T(8,128)(2,1)} %param.13) | copy-start | bytes 1769476
  14.6 83.5 %all-to-all-start = ((bf16[1,4,1,2,2,384,384]{5,6,4,3,2,0,1:T(8,128)(2,1)}), bf16[1,4,1,2,2,384,384]{5,6,4,3,2,0,1:T(8,128)(2,1)}, u32[]{:S(2)}, u32[]{:S(2)}) async-start(bf16[1,4,1,2,2,384,384]{5,6,4,3,2,0,1:T(8,128)(2,1)} %copy.195), calls=%async_computation | async-start | bytes 9437184 | tf_op jit(solution)/shard_map/all_to_all | solution.py:155
  19.7 108.0 %all-gather.5.cloned.1.call-start = ((), (), s32[]{:S(2)}) async-start(), calls=%async_computation.4 | async-start | bytes 2949120 | tf_op jit(solution)/shard_map/all_gather | solution.py:160
  98.1 107.8 %collective-permute-start = (bf16[1,1,4,2,2,384,384]{5,6,4,3,2,1,0:T(8,128)(2,1)}, bf16[1,1,4,2,2,384,384]{5,6,4,3,2,1,0:T(8,128)(2,1)}, u32[]{:S(2)}, u32[]{:S(2)}) collective-permute-start(bf16[1,1,4,2,2,384,384]{5,6,4,3,2,1,0:T(8,128)(2,1)} %bitcast.41), channel_id=1, source_target_pairs={{0,1},{1,2},{2,3},{3,4},{4,5},{5,6},{6,7},{7,0},{8,9},{9,10},{10,1... | collective-permute-start | bytes 14155784 | tf_op jit(solution)/shard_map/ppermute | solution.py:13
  99.6 106.8 %collective-permute-start.1 = (bf16[1,1,4,2,2,384,384]{5,6,4,3,2,1,0:T(8,128)(2,1)}, bf16[1,1,4,2,2,384,384]{5,6,4,3,2,1,0:T(8,128)(2,1)}, u32[]{:S(2)}, u32[]{:S(2)}) collective-permute-start(bf16[1,1,4,2,2,384,384]{5,6,4,3,2,1,0:T(8,128)(2,1)} %bitcast.41), channel_id=1, source_target_pairs={{0,2},{1,3},{2,4},{3,5},{4,6},{5,7},{6,0},{7,1},{8,10},{9,11},{10,... | collective-permute-start | bytes 14155784 | tf_op jit(solution)/shard_map/ppermute | solution.py:13
  101.1 204.6 %collective-permute-start.2 = (bf16[1,1,4,2,2,384,384]{5,6,4,3,2,1,0:T(8,128)(2,1)}, bf16[1,1,4,2,2,384,384]{5,6,4,3,2,1,0:T(8,128)(2,1)}, u32[]{:S(2)}, u32[]{:S(2)}) collective-permute-start(bf16[1,1,4,2,2,384,384]{5,6,4,3,2,1,0:T(8,128)(2,1)} %bitcast.41), channel_id=1, source_target_pairs={{0,7},{1,0},{2,1},{3,2},{4,3},{5,4},{6,5},{7,6},{8,15},{9,8},{10,9... | collective-permute-start | bytes 14155784 | tf_op jit(solution)/shard_map/ppermute | solution.py:13
  104.3 303.0 %collective-permute-start.3 = (bf16[1,1,4,2,2,384,384]{5,6,4,3,2,1,0:T(8,128)(2,1)}, bf16[1,1,4,2,2,384,384]{5,6,4,3,2,1,0:T(8,128)(2,1)}, u32[]{:S(2)}, u32[]{:S(2)}) collective-permute-start(bf16[1,1,4,2,2,384,384]{5,6,4,3,2,1,0:T(8,128)(2,1)} %bitcast.41), channel_id=1, source_target_pairs={{0,6},{1,7},{2,0},{3,1},{4,2},{5,3},{6,4},{7,5},{8,14},{9,15},{10,... | collective-permute-start | bytes 14155784 | tf_op jit(solution)/shard_map/ppermute | solution.py:13
  108.0 1.6 copy-start.14
  108.1 3.5 copy-start.15
  108.1 8.8 %copy-start.17 = (f32[4]{0:T(128)S(1)}, f32[4]{0:T(128)}, u32[]{:S(2)}) copy-start(f32[4]{0:T(128)} %param.17) | copy-start | bytes 52
  108.1 8.8 %copy-start.18 = (s32[1,2]{1,0:T(1,128)S(1)}, s32[1,2]{1,0:T(1,128)}, u32[]{:S(2)}) copy-start(s32[1,2]{1,0:T(1,128)} %param.16) | copy-start | bytes 28
  423.6 1.0 copy-start.11
  423.6 1.0 copy-start.12
  429.8 1.7 copy-start
  434.8 1.0 copy-start.9
  434.8 1.0 copy-start.10
  444.1 1.0 copy-start.8
  450.2 1.4 copy-start.1
  453.5 1.0 copy-start.6
  458.4 1.0 copy-start.4
  462.9 32.1 %all-to-all-start.2 = ((bf16[1,1,4,2,384,384]{4,5,3,1,0,2:T(8,128)(2,1)}), bf16[1,1,4,2,384,384]{4,5,3,1,0,2:T(8,128)(2,1)S(1)}, u32[]{:S(2)}, u32[]{:S(2)}) async-start(bf16[1,1,4,2,384,384]{4,5,3,1,0,2:T(8,128)(2,1)} %maximum_bitcast_fusion.1), calls=%async_computation.2 | async-start | bytes 4718592 | tf_op jit(solution)/shard_map/all_to_all | solution.py:176
  466.5 1.8 copy-start.2
  494.9 33.1 %all-to-all-start.1 = ((bf16[1,1,4,2,384,384]{4,5,3,1,0,2:T(8,128)(2,1)}), bf16[1,1,4,2,384,384]{4,5,3,1,0,2:T(8,128)(2,1)}, u32[]{:S(2)}, u32[]{:S(2)}) async-start(bf16[1,1,4,2,384,384]{4,5,3,1,0,2:T(8,128)(2,1)} %maximum_bitcast_fusion), calls=%async_computation.1 | async-start | bytes 4718592 | tf_op jit(solution)/shard_map/all_to_all | solution.py:173
  (4 other events, 3.4 us)
Sparse Core Ops, SparseCore 0:
  9.5 38.0 all-gather.2
  49.2 35.9 all-gather.4

commit v2 on v1

--- a/solution.py
+++ b/solution.py
@@ -152,14 +152,21 @@
     energies, onsite, hamiltonian, hopping, contact, previous, neighbours, mode_index, mode_strength
 ):
     position = lax.axis_index("slab")
-    regrouped = lax.all_to_all(previous, "slab", split_axis=1, concat_axis=2, tiled=True)
-    phonon_all = cycle_phonon(regrouped, neighbours, mode_index, mode_strength)
+    kind_list = []
+    for kind in range(2):
+        part_list = []
+        for part in range(2):
+            piece = previous[:, :, :, kind : kind + 1, part : part + 1]
+            regrouped = lax.all_to_all(piece, "slab", split_axis=1, concat_axis=2, tiled=True)
+            part_list.append(cycle_phonon(regrouped, neighbours, mode_index, mode_strength))
+        kind_list.append(jnp.concatenate(part_list, axis=3))
+    phonon_all = jnp.concatenate(kind_list, axis=2)
     level_whole = lax.all_gather(onsite, "slab", axis=1, tiled=True)
     hamilton_whole, coupling_whole = (
         lax.all_gather(hamiltonian, "slab", axis=1, tiled=True),
         lax.all_gather(hopping, "slab", axis=1, tiled=True),
     )
-    local_count = regrouped.shape[1]
+    local_count = phonon_all.shape[0]
     local_energies = lax.dynamic_slice_in_dim(energies, position * local_count, local_count, 0)
     initial = starting_blocks(contact, local_energies)
 

time: 542 us -> 530 us (0.978)
  the two profiles are of different devices: /device:TPU:0 before, /device:TPU:12 now
where the time goes in v2:
time: 530 us; the launch traced here: 521 us
  waiting for transfers between devices  241 us (45%)
  starting transfers between devices  100 us (19%)
  local copies, waits for them, and re-layouts  54 us (10%)
  other arithmetic  38.6 us (7%)
  blocking collectives  37 us (7%)
  matrix products  32.4 us (6%)
  between operations  17.5 us (3%)
    ppermute x16, waiting for transfers between devices, from_behind(): lax.ppermute(value, axis, [(i, (i + by) % peers) for i in range(peers)])  183 us
    ppermute x16, starting transfers between devices, from_behind(): lax.ppermute(value, axis, [(i, (i + by) % peers) for i in range(peers)])  79.3 us
    unnamed x105, local copies, waits for them, and re-layouts  39.1 us
    all_to_all x1, blocking collectives, body(): lax.all_to_all(piece, 'slab', split_axis=1, concat_axis=2, tiled=True)  31.6 us
    all_to_all x1, waiting for transfers between devices, body(): lax.all_to_all(as_sent(lesser_local[None]), 'slab', split_axis=2, concat_...  24.2 us
    all_to_all x1, waiting for transfers between devices, body(): lax.all_to_all(as_sent(retarded_local[None]), 'slab', split_axis=2, conca...  21.8 us
    dot_general x8, matrix products, mul_adjoint(): jnp.einsum('...pij,qkj->...pqik', first_op, second_op, preferred_element_...  13.1 us
    add x4, other arithmetic, cycle_phonon(): strength[0] * behind[0].astype(jnp.float32)  12.9 us
  transfers between devices with their start and end apart: 23, of which 16 were waited for; matrix products, arithmetic and copies ran while one was open for 10% of the time, Pallas kernels for 0%

profile of v2, /device:TPU:12, one launch (start us, length us, event | category | flops | bytes accessed | tf_op | source)
XLA Modules:
  0.0 521.3 jit_solution(7655370063930717698)
XLA Ops:
  14.3 31.6 %all_to_all.72 = bf16[1,4,1,1,1,384,384]{5,6,4,3,2,0,1:T(8,128)(2,1)} all-to-all(bf16[1,4,1,1,1,384,384]{5,6,4,3,2,0,1:T(8,128)(2,1)} %copy.379), channel_id=1, replica_groups=mesh['slab'=4,'kt'=8] {'slab'}, dimensions={1} | all-to-all | bytes 2359296 | tf_op jit(solution)/shard_map/all_to_all | solution.py:160
  47.9 4.3 all-to-all-start.2
  56.7 11.4 %all-to-all-done.2 = bf16[1,4,1,1,1,384,384]{5,6,4,3,2,0,1:T(8,128)(2,1)} async-done(((bf16[1,4,1,1,1,384,384]{5,6,4,3,2,0,1:T(8,128)(2,1)}), bf16[1,4,1,1,1,384,384]{5,6,4,3,2,0,1:T(8,128)(2,1)}, u32[]{:S(2)}, u32[]{:S(2)}) %all-to-all-start.2) | async-done | bytes 1179680 | tf_op jit(solution)/shard_map/all_to_all | solution.py:160
  69.6 6.5 %collective-permute-done.14 = bf16[1,1,4,1,1,384,384]{5,6,2,4,3,1,0:T(8,128)(2,1)} collective-permute-done((bf16[1,1,4,1,1,384,384]{5,6,2,4,3,1,0:T(8,128)(2,1)}, bf16[1,1,4,1,1,384,384]{5,6,2,4,3,1,0:T(8,128)(2,1)}, u32[]{:S(2)}, u32[]{:S(2)}) %collective-permute-start.14) | collective-permute-done | bytes 1179680 | tf_op jit(solution)/shard_map/ppermute | solution.py:13
  78.0 4.3 all-to-all-start.1
  82.4 20.3 %collective-permute-start.8 = (bf16[1,1,4,1,1,384,384]{5,6,2,4,3,1,0:T(8,128)(2,1)}, bf16[1,1,4,1,1,384,384]{5,6,2,4,3,1,0:T(8,128)(2,1)}, u32[]{:S(2)}, u32[]{:S(2)}) collective-permute-start(bf16[1,1,4,1,1,384,384]{5,6,2,4,3,1,0:T(8,128)(2,1)} %bitcast.47), channel_id=1, source_target_pairs={{0,1},{1,2},{2,3},{3,4},{4,5},{5,6},{6,7},{7,0},{8,9},{9,10},{10,1... | collective-permute-start | bytes 3538952 | tf_op jit(solution)/shard_map/ppermute | solution.py:13
  104.3 4.3 all-to-all-start
  112.0 22.0 %collective-permute-done.13 = bf16[1,1,4,1,1,384,384]{5,6,2,4,3,1,0:T(8,128)(2,1)} collective-permute-done((bf16[1,1,4,1,1,384,384]{5,6,2,4,3,1,0:T(8,128)(2,1)}, bf16[1,1,4,1,1,384,384]{5,6,2,4,3,1,0:T(8,128)(2,1)}, u32[]{:S(2)}, u32[]{:S(2)}) %collective-permute-start.13) | collective-permute-done | bytes 1179680 | tf_op jit(solution)/shard_map/ppermute | solution.py:13
  133.9 18.0 %collective-permute-done.10 = bf16[1,1,4,1,1,384,384]{5,6,2,4,3,1,0:T(8,128)(2,1)} collective-permute-done((bf16[1,1,4,1,1,384,384]{5,6,2,4,3,1,0:T(8,128)(2,1)}, bf16[1,1,4,1,1,384,384]{5,6,2,4,3,1,0:T(8,128)(2,1)}, u32[]{:S(2)}, u32[]{:S(2)}) %collective-permute-start.10) | collective-permute-done | bytes 1179680 | tf_op jit(solution)/shard_map/ppermute | solution.py:13
  152.4 5.0 collective-permute-done.11
  157.4 21.3 %collective-permute-start.4 = (bf16[1,1,4,1,1,384,384]{5,6,2,4,3,1,0:T(8,128)(2,1)}, bf16[1,1,4,1,1,384,384]{5,6,2,4,3,1,0:T(8,128)(2,1)}, u32[]{:S(2)}, u32[]{:S(2)}) collective-permute-start(bf16[1,1,4,1,1,384,384]{5,6,2,4,3,1,0:T(8,128)(2,1)} %bitcast.45), channel_id=1, source_target_pairs={{0,1},{1,2},{2,3},{3,4},{4,5},{5,6},{6,7},{7,0},{8,9},{9,10},{10,1... | collective-permute-start | bytes 3538952 | tf_op jit(solution)/shard_map/ppermute | solution.py:13
  184.2 5.3 %all_gather.9 = f32[1,4,384]{2,0,1:T(1,128)S(1)} all-gather(f32[1,1,384]{2,0,1:T(1,128)S(1)} %bitcast.947), channel_id=1, replica_groups=mesh['slab'=4,'kt'=8] {'slab'}, dimensions={1}, use_global_device_ids=true | all-gather | bytes 7680 | tf_op jit(solution)/shard_map/all_gather | solution.py:164
  194.5 15.3 %collective-permute-done.9 = bf16[1,1,4,1,1,384,384]{5,6,2,4,3,1,0:T(8,128)(2,1)} collective-permute-done((bf16[1,1,4,1,1,384,384]{5,6,2,4,3,1,0:T(8,128)(2,1)}, bf16[1,1,4,1,1,384,384]{5,6,2,4,3,1,0:T(8,128)(2,1)}, u32[]{:S(2)}, u32[]{:S(2)}) %collective-permute-start.9) | collective-permute-done | bytes 1179680 | tf_op jit(solution)/shard_map/ppermute | solution.py:13
  209.8 17.9 %collective-permute-done.6 = bf16[1,1,4,1,1,384,384]{5,6,2,4,3,1,0:T(8,128)(2,1)} collective-permute-done((bf16[1,1,4,1,1,384,384]{5,6,2,4,3,1,0:T(8,128)(2,1)}, bf16[1,1,4,1,1,384,384]{5,6,2,4,3,1,0:T(8,128)(2,1)}, u32[]{:S(2)}, u32[]{:S(2)}) %collective-permute-start.6) | collective-permute-done | bytes 1179680 | tf_op jit(solution)/shard_map/ppermute | solution.py:13
  228.3 4.9 collective-permute-done.7
  233.2 21.4 %collective-permute-start = (bf16[1,1,4,1,1,384,384]{5,6,2,4,3,1,0:T(8,128)(2,1)}, bf16[1,1,4,1,1,384,384]{5,6,2,4,3,1,0:T(8,128)(2,1)S(1)}, u32[]{:S(2)}, u32[]{:S(2)}) collective-permute-start(bf16[1,1,4,1,1,384,384]{5,6,2,4,3,1,0:T(8,128)(2,1)} %bitcast.41), channel_id=1, source_target_pairs={{0,1},{1,2},{2,3},{3,4},{4,5},{5,6},{6,7},{7,0},{8,9},{9,10},{10,1... | collective-permute-start | bytes 3538952 | tf_op jit(solution)/shard_map/ppermute | solution.py:13
  267.6 18.1 %collective-permute-done.5 = bf16[1,1,4,1,1,384,384]{5,6,2,4,3,1,0:T(8,128)(2,1)} collective-permute-done((bf16[1,1,4,1,1,384,384]{5,6,2,4,3,1,0:T(8,128)(2,1)}, bf16[1,1,4,1,1,384,384]{5,6,2,4,3,1,0:T(8,128)(2,1)}, u32[]{:S(2)}, u32[]{:S(2)}) %collective-permute-start.5) | collective-permute-done | bytes 1179680 | tf_op jit(solution)/shard_map/ppermute | solution.py:13
  289.4 14.1 %collective-permute-done.2 = bf16[1,1,4,1,1,384,384]{5,6,2,4,3,1,0:T(8,128)(2,1)S(1)} collective-permute-done((bf16[1,1,4,1,1,384,384]{5,6,2,4,3,1,0:T(8,128)(2,1)}, bf16[1,1,4,1,1,384,384]{5,6,2,4,3,1,0:T(8,128)(2,1)S(1)}, u32[]{:S(2)}, u32[]{:S(2)}) %collective-permute-start.2) | collective-permute-done | bytes 1179680 | tf_op jit(solution)/shard_map/ppermute | solution.py:13
  303.5 4.8 collective-permute-done.3
  308.3 26.4 %collective-permute-done = bf16[1,1,4,1,1,384,384]{5,6,2,4,3,1,0:T(8,128)(2,1)S(1)} collective-permute-done((bf16[1,1,4,1,1,384,384]{5,6,2,4,3,1,0:T(8,128)(2,1)}, bf16[1,1,4,1,1,384,384]{5,6,2,4,3,1,0:T(8,128)(2,1)S(1)}, u32[]{:S(2)}, u32[]{:S(2)}) %collective-permute-start) | collective-permute-done | bytes 1179680 | tf_op jit(solution)/shard_map/ppermute | solution.py:13
  334.7 26.3 %collective-permute-done.1 = bf16[1,1,4,1,1,384,384]{5,6,2,4,3,1,0:T(8,128)(2,1)S(1)} collective-permute-done((bf16[1,1,4,1,1,384,384]{5,6,2,4,3,1,0:T(8,128)(2,1)}, bf16[1,1,4,1,1,384,384]{5,6,2,4,3,1,0:T(8,128)(2,1)S(1)}, u32[]{:S(2)}, u32[]{:S(2)}) %collective-permute-start.1) | collective-permute-done | bytes 1179680 | tf_op jit(solution)/shard_map/ppermute | solution.py:13
  446.3 4.5 all-to-all-start.4
  457.6 21.8 %all-to-all-done.4 = bf16[1,1,4,2,384,384]{4,5,3,1,0,2:T(8,128)(2,1)} async-done(((bf16[1,1,4,2,384,384]{4,5,3,1,0,2:T(8,128)(2,1)}), bf16[1,1,4,2,384,384]{4,5,3,1,0,2:T(8,128)(2,1)}, u32[]{:S(2)}, u32[]{:S(2)}) %all-to-all-start.4) | async-done | bytes 2359328 | tf_op jit(solution)/shard_map/all_to_all | solution.py:180
  487.2 24.2 %all-to-all-done.5 = bf16[1,1,4,2,384,384]{4,5,3,1,0,2:T(8,128)(2,1)S(1)} async-done(((bf16[1,1,4,2,384,384]{4,5,3,1,0,2:T(8,128)(2,1)}), bf16[1,1,4,2,384,384]{4,5,3,1,0,2:T(8,128)(2,1)S(1)}, u32[]{:S(2)}, u32[]{:S(2)}) %all-to-all-start.5) | async-done | bytes 2359328 | tf_op jit(solution)/shard_map/all_to_all | solution.py:183
  (244 shorter events, 149.9 us)
Async XLA Ops:
  7.2 361.2 %all-gather.5.cloned.1.call-start = ((), (), s32[]{:S(2)}) async-start(), calls=%async_computation.7 | async-start | bytes 2949120 | tf_op jit(solution)/shard_map/all_gather | solution.py:167
  45.9 30.1 %collective-permute-start.14 = (bf16[1,1,4,1,1,384,384]{5,6,2,4,3,1,0:T(8,128)(2,1)}, bf16[1,1,4,1,1,384,384]{5,6,2,4,3,1,0:T(8,128)(2,1)}, u32[]{:S(2)}, u32[]{:S(2)}) collective-permute-start(bf16[1,1,4,1,1,384,384]{5,6,2,4,3,1,0:T(8,128)(2,1)} %bitcast.50), channel_id=1, source_target_pairs={{0,7},{1,0},{2,1},{3,2},{4,3},{5,4},{6,5},{7,6},{8,15},{9,8},{10,9... | collective-permute-start | bytes 3538952 | tf_op jit(solution)/shard_map/ppermute | solution.py:13
  47.9 20.2 %all-to-all-start.2 = ((bf16[1,4,1,1,1,384,384]{5,6,4,3,2,0,1:T(8,128)(2,1)}), bf16[1,4,1,1,1,384,384]{5,6,4,3,2,0,1:T(8,128)(2,1)}, u32[]{:S(2)}, u32[]{:S(2)}) async-start(bf16[1,4,1,1,1,384,384]{5,6,4,3,2,0,1:T(8,128)(2,1)} %copy.378), calls=%async_computation.2 | async-start | bytes 2359296 | tf_op jit(solution)/shard_map/all_to_all | solution.py:160
  52.2 30.1 %collective-permute-start.15 = (bf16[1,1,4,1,1,384,384]{5,6,2,4,3,1,0:T(8,128)(2,1)}, bf16[1,1,4,1,1,384,384]{5,6,2,4,3,1,0:T(8,128)(2,1)S(1)}, u32[]{:S(2)}, u32[]{:S(2)}) collective-permute-start(bf16[1,1,4,1,1,384,384]{5,6,2,4,3,1,0:T(8,128)(2,1)} %bitcast.50), channel_id=1, source_target_pairs={{0,6},{1,7},{2,0},{3,1},{4,2},{5,3},{6,4},{7,5},{8,14},{9,15},{10,... | collective-permute-start | bytes 3538952 | tf_op jit(solution)/shard_map/ppermute | solution.py:13
  52.8 55.8 %collective-permute-start.12 = (bf16[1,1,4,1,1,384,384]{5,6,2,4,3,1,0:T(8,128)(2,1)}, bf16[1,1,4,1,1,384,384]{5,6,2,4,3,1,0:T(8,128)(2,1)}, u32[]{:S(2)}, u32[]{:S(2)}) collective-permute-start(bf16[1,1,4,1,1,384,384]{5,6,2,4,3,1,0:T(8,128)(2,1)} %bitcast.50), channel_id=1, source_target_pairs={{0,1},{1,2},{2,3},{3,4},{4,5},{5,6},{6,7},{7,0},{8,9},{9,10},{10,1... | collective-permute-start | bytes 3538952 | tf_op jit(solution)/shard_map/ppermute | solution.py:13
  55.2 78.7 %collective-permute-start.13 = (bf16[1,1,4,1,1,384,384]{5,6,2,4,3,1,0:T(8,128)(2,1)}, bf16[1,1,4,1,1,384,384]{5,6,2,4,3,1,0:T(8,128)(2,1)}, u32[]{:S(2)}, u32[]{:S(2)}) collective-permute-start(bf16[1,1,4,1,1,384,384]{5,6,2,4,3,1,0:T(8,128)(2,1)} %bitcast.50), channel_id=1, source_target_pairs={{0,2},{1,3},{2,4},{3,5},{4,6},{5,7},{6,0},{7,1},{8,10},{9,11},{10,... | collective-permute-start | bytes 3538952 | tf_op jit(solution)/shard_map/ppermute | solution.py:13
  68.1 83.8 %collective-permute-start.10 = (bf16[1,1,4,1,1,384,384]{5,6,2,4,3,1,0:T(8,128)(2,1)}, bf16[1,1,4,1,1,384,384]{5,6,2,4,3,1,0:T(8,128)(2,1)}, u32[]{:S(2)}, u32[]{:S(2)}) collective-permute-start(bf16[1,1,4,1,1,384,384]{5,6,2,4,3,1,0:T(8,128)(2,1)} %bitcast.47), channel_id=1, source_target_pairs={{0,7},{1,0},{2,1},{3,2},{4,3},{5,4},{6,5},{7,6},{8,15},{9,8},{10,9... | collective-permute-start | bytes 3538952 | tf_op jit(solution)/shard_map/ppermute | solution.py:13
  76.0 81.4 %collective-permute-start.11 = (bf16[1,1,4,1,1,384,384]{5,6,2,4,3,1,0:T(8,128)(2,1)}, bf16[1,1,4,1,1,384,384]{5,6,2,4,3,1,0:T(8,128)(2,1)}, u32[]{:S(2)}, u32[]{:S(2)}) collective-permute-start(bf16[1,1,4,1,1,384,384]{5,6,2,4,3,1,0:T(8,128)(2,1)} %bitcast.47), channel_id=1, source_target_pairs={{0,6},{1,7},{2,0},{3,1},{4,2},{5,3},{6,4},{7,5},{8,14},{9,15},{10,... | collective-permute-start | bytes 3538952 | tf_op jit(solution)/shard_map/ppermute | solution.py:13
  78.0 26.3 %all-to-all-start.1 = ((bf16[1,4,1,1,1,384,384]{5,6,4,3,2,0,1:T(8,128)(2,1)}), bf16[1,4,1,1,1,384,384]{5,6,4,3,2,0,1:T(8,128)(2,1)}, u32[]{:S(2)}, u32[]{:S(2)}) async-start(bf16[1,4,1,1,1,384,384]{5,6,4,3,2,0,1:T(8,128)(2,1)} %copy.377), calls=%async_computation.1 | async-start | bytes 2359296 | tf_op jit(solution)/shard_map/all_to_all | solution.py:160
  82.3 292.6 %all-gather.3.cloned.1.call-start = ((), (), s32[]{:S(2)}) async-start(), calls=%async_computation.6 | async-start | bytes 2949120 | tf_op jit(solution)/shard_map/all_gather | solution.py:166
  82.4 21.8 %copy-start.39 = (bf16[1,1,4,1,1,384,384]{5,6,2,4,3,1,0:T(8,128)(2,1)}, bf16[1,1,4,1,1,384,384]{5,6,2,4,3,1,0:T(8,128)(2,1)S(1)}, u32[]{:S(2)}) copy-start(bf16[1,1,4,1,1,384,384]{5,6,2,4,3,1,0:T(8,128)(2,1)S(1)} %collective-permute-done.15) | copy-start | bytes 3538948
  82.4 108.6 %collective-permute-start.8 = (bf16[1,1,4,1,1,384,384]{5,6,2,4,3,1,0:T(8,128)(2,1)}, bf16[1,1,4,1,1,384,384]{5,6,2,4,3,1,0:T(8,128)(2,1)}, u32[]{:S(2)}, u32[]{:S(2)}) collective-permute-start(bf16[1,1,4,1,1,384,384]{5,6,2,4,3,1,0:T(8,128)(2,1)} %bitcast.47), channel_id=1, source_target_pairs={{0,1},{1,2},{2,3},{3,4},{4,5},{5,6},{6,7},{7,0},{8,9},{9,10},{10,1... | collective-permute-start | bytes 3538952 | tf_op jit(solution)/shard_map/ppermute | solution.py:13
  104.3 90.2 %all-to-all-start = ((bf16[1,4,1,1,1,384,384]{5,6,4,3,2,0,1:T(8,128)(2,1)}), bf16[1,4,1,1,1,384,384]{5,6,4,3,2,0,1:T(8,128)(2,1)}, u32[]{:S(2)}, u32[]{:S(2)}) async-start(bf16[1,4,1,1,1,384,384]{5,6,4,3,2,0,1:T(8,128)(2,1)} %copy.376), calls=%async_computation | async-start | bytes 2359296 | tf_op jit(solution)/shard_map/all_to_all | solution.py:160
  108.6 101.2 %collective-permute-start.9 = (bf16[1,1,4,1,1,384,384]{5,6,2,4,3,1,0:T(8,128)(2,1)}, bf16[1,1,4,1,1,384,384]{5,6,2,4,3,1,0:T(8,128)(2,1)}, u32[]{:S(2)}, u32[]{:S(2)}) collective-permute-start(bf16[1,1,4,1,1,384,384]{5,6,2,4,3,1,0:T(8,128)(2,1)} %bitcast.47), channel_id=1, source_target_pairs={{0,2},{1,3},{2,4},{3,5},{4,6},{5,7},{6,0},{7,1},{8,10},{9,11},{10,... | collective-permute-start | bytes 3538952 | tf_op jit(solution)/shard_map/ppermute | solution.py:13
  133.9 93.8 %collective-permute-start.6 = (bf16[1,1,4,1,1,384,384]{5,6,2,4,3,1,0:T(8,128)(2,1)}, bf16[1,1,4,1,1,384,384]{5,6,2,4,3,1,0:T(8,128)(2,1)}, u32[]{:S(2)}, u32[]{:S(2)}) collective-permute-start(bf16[1,1,4,1,1,384,384]{5,6,2,4,3,1,0:T(8,128)(2,1)} %bitcast.45), channel_id=1, source_target_pairs={{0,7},{1,0},{2,1},{3,2},{4,3},{5,4},{6,5},{7,6},{8,15},{9,8},{10,9... | collective-permute-start | bytes 3538952 | tf_op jit(solution)/shard_map/ppermute | solution.py:13
  151.9 81.3 %collective-permute-start.7 = (bf16[1,1,4,1,1,384,384]{5,6,2,4,3,1,0:T(8,128)(2,1)}, bf16[1,1,4,1,1,384,384]{5,6,2,4,3,1,0:T(8,128)(2,1)}, u32[]{:S(2)}, u32[]{:S(2)}) collective-permute-start(bf16[1,1,4,1,1,384,384]{5,6,2,4,3,1,0:T(8,128)(2,1)} %bitcast.45), channel_id=1, source_target_pairs={{0,6},{1,7},{2,0},{3,1},{4,2},{5,3},{6,4},{7,5},{8,14},{9,15},{10,... | collective-permute-start | bytes 3538952 | tf_op jit(solution)/shard_map/ppermute | solution.py:13
  157.4 101.5 %collective-permute-start.4 = (bf16[1,1,4,1,1,384,384]{5,6,2,4,3,1,0:T(8,128)(2,1)}, bf16[1,1,4,1,1,384,384]{5,6,2,4,3,1,0:T(8,128)(2,1)}, u32[]{:S(2)}, u32[]{:S(2)}) collective-permute-start(bf16[1,1,4,1,1,384,384]{5,6,2,4,3,1,0:T(8,128)(2,1)} %bitcast.45), channel_id=1, source_target_pairs={{0,1},{1,2},{2,3},{3,4},{4,5},{5,6},{6,7},{7,0},{8,9},{9,10},{10,1... | collective-permute-start | bytes 3538952 | tf_op jit(solution)/shard_map/ppermute | solution.py:13
  191.0 94.8 %collective-permute-start.5 = (bf16[1,1,4,1,1,384,384]{5,6,2,4,3,1,0:T(8,128)(2,1)}, bf16[1,1,4,1,1,384,384]{5,6,2,4,3,1,0:T(8,128)(2,1)}, u32[]{:S(2)}, u32[]{:S(2)}) collective-permute-start(bf16[1,1,4,1,1,384,384]{5,6,2,4,3,1,0:T(8,128)(2,1)} %bitcast.45), channel_id=1, source_target_pairs={{0,2},{1,3},{2,4},{3,5},{4,6},{5,7},{6,0},{7,1},{8,10},{9,11},{10,... | collective-permute-start | bytes 3538952 | tf_op jit(solution)/shard_map/ppermute | solution.py:13
  209.8 93.6 %collective-permute-start.2 = (bf16[1,1,4,1,1,384,384]{5,6,2,4,3,1,0:T(8,128)(2,1)}, bf16[1,1,4,1,1,384,384]{5,6,2,4,3,1,0:T(8,128)(2,1)S(1)}, u32[]{:S(2)}, u32[]{:S(2)}) collective-permute-start(bf16[1,1,4,1,1,384,384]{5,6,2,4,3,1,0:T(8,128)(2,1)} %bitcast.41), channel_id=1, source_target_pairs={{0,7},{1,0},{2,1},{3,2},{4,3},{5,4},{6,5},{7,6},{8,15},{9,8},{10,9... | collective-permute-start | bytes 3538952 | tf_op jit(solution)/shard_map/ppermute | solution.py:13
  227.7 80.5 %collective-permute-start.3 = (bf16[1,1,4,1,1,384,384]{5,6,2,4,3,1,0:T(8,128)(2,1)}, bf16[1,1,4,1,1,384,384]{5,6,2,4,3,1,0:T(8,128)(2,1)S(1)}, u32[]{:S(2)}, u32[]{:S(2)}) collective-permute-start(bf16[1,1,4,1,1,384,384]{5,6,2,4,3,1,0:T(8,128)(2,1)} %bitcast.41), channel_id=1, source_target_pairs={{0,6},{1,7},{2,0},{3,1},{4,2},{5,3},{6,4},{7,5},{8,14},{9,15},{10,... | collective-permute-start | bytes 3538952 | tf_op jit(solution)/shard_map/ppermute | solution.py:13
  233.2 101.5 %collective-permute-start = (bf16[1,1,4,1,1,384,384]{5,6,2,4,3,1,0:T(8,128)(2,1)}, bf16[1,1,4,1,1,384,384]{5,6,2,4,3,1,0:T(8,128)(2,1)S(1)}, u32[]{:S(2)}, u32[]{:S(2)}) collective-permute-start(bf16[1,1,4,1,1,384,384]{5,6,2,4,3,1,0:T(8,128)(2,1)} %bitcast.41), channel_id=1, source_target_pairs={{0,1},{1,2},{2,3},{3,4},{4,5},{5,6},{6,7},{7,0},{8,9},{9,10},{10,1... | collective-permute-start | bytes 3538952 | tf_op jit(solution)/shard_map/ppermute | solution.py:13
  258.9 102.1 %collective-permute-start.1 = (bf16[1,1,4,1,1,384,384]{5,6,2,4,3,1,0:T(8,128)(2,1)}, bf16[1,1,4,1,1,384,384]{5,6,2,4,3,1,0:T(8,128)(2,1)S(1)}, u32[]{:S(2)}, u32[]{:S(2)}) collective-permute-start(bf16[1,1,4,1,1,384,384]{5,6,2,4,3,1,0:T(8,128)(2,1)} %bitcast.41), channel_id=1, source_target_pairs={{0,2},{1,3},{2,4},{3,5},{4,6},{5,7},{6,0},{7,1},{8,10},{9,11},{10,... | collective-permute-start | bytes 3538952 | tf_op jit(solution)/shard_map/ppermute | solution.py:13
  446.3 33.1 %all-to-all-start.4 = ((bf16[1,1,4,2,384,384]{4,5,3,1,0,2:T(8,128)(2,1)}), bf16[1,1,4,2,384,384]{4,5,3,1,0,2:T(8,128)(2,1)}, u32[]{:S(2)}, u32[]{:S(2)}) async-start(bf16[1,1,4,2,384,384]{4,5,3,1,0,2:T(8,128)(2,1)} %maximum_bitcast_fusion), calls=%async_computation.4 | async-start | bytes 4718592 | tf_op jit(solution)/shard_map/all_to_all | solution.py:180
  479.3 32.1 %all-to-all-start.5 = ((bf16[1,1,4,2,384,384]{4,5,3,1,0,2:T(8,128)(2,1)}), bf16[1,1,4,2,384,384]{4,5,3,1,0,2:T(8,128)(2,1)S(1)}, u32[]{:S(2)}, u32[]{:S(2)}) async-start(bf16[1,1,4,2,384,384]{4,5,3,1,0,2:T(8,128)(2,1)} %maximum_bitcast_fusion.1), calls=%async_computation.5 | async-start | bytes 4718592 | tf_op jit(solution)/shard_map/all_to_all | solution.py:183
  (44 other events, 94.2 us)
Sparse Core Ops, SparseCore 0:
  9.5 36.8 all-gather.4
  102.8 45.5 all-gather.2

commit v3 on v2

--- a/solution.py
+++ b/solution.py
@@ -128,9 +128,11 @@
         jnp.where(mode_index[0][:, None] == mode_table[None, :], mode_strength[None, :], 0.0),
         axis=1,
     )
-    return strength[0] * behind[0].astype(jnp.float32) + strength[1] * forward[0].astype(
-        jnp.float32
-    )
+    return strength, behind, forward
+
+
+def weigh(strength, behind, forward):
+    return strength[0] * behind.astype(jnp.float32) + strength[1] * forward.astype(jnp.float32)
 
 
 def starting_blocks(contact, energy_list):
@@ -157,8 +159,26 @@
         part_list = []
         for part in range(2):
             piece = previous[:, :, :, kind : kind + 1, part : part + 1]
-            regrouped = lax.all_to_all(piece, "slab", split_axis=1, concat_axis=2, tiled=True)
-            part_list.append(cycle_phonon(regrouped, neighbours, mode_index, mode_strength))
+            if kind == 0 and part == 0:
+                strength, behind, forward = cycle_phonon(
+                    piece, neighbours, mode_index, mode_strength
+                )
+                chosen = lax.all_to_all(
+                    jnp.stack([behind, forward], axis=1),
+                    "slab",
+                    split_axis=2,
+                    concat_axis=3,
+                    tiled=True,
+                )
+                part_list.append(weigh(strength, chosen[0, 0], chosen[0, 1]))
+            else:
+                regrouped = lax.all_to_all(
+                    piece, "slab", split_axis=1, concat_axis=2, tiled=True
+                )
+                strength, behind, forward = cycle_phonon(
+                    regrouped, neighbours, mode_index, mode_strength
+                )
+                part_list.append(weigh(strength, behind[0], forward[0]))
         kind_list.append(jnp.concatenate(part_list, axis=3))
     phonon_all = jnp.concatenate(kind_list, axis=2)
     level_whole = lax.all_gather(onsite, "slab", axis=1, tiled=True)
@@ -176,15 +196,14 @@
         )
 
     retarded_local, lesser_local, unused = jax.vmap(run_whole)(initial, local_energies, phonon_all)
-    retarded_all, lesser_all = (
-        lax.all_to_all(
-            as_sent(retarded_local[None]), "slab", split_axis=2, concat_axis=1, tiled=True
-        ),
-        lax.all_to_all(
-            as_sent(lesser_local[None]), "slab", split_axis=2, concat_axis=1, tiled=True
-        ),
-    )
-    return (retarded_all, lesser_all)
+    both_all = lax.all_to_all(
+        as_sent(jnp.stack([retarded_local, lesser_local])[:, None]),
+        "slab",
+        split_axis=3,
+        concat_axis=2,
+        tiled=True,
+    )
+    return (both_all[0], both_all[1])
 
 
 def solution(mesh):

time: 530 us -> 507 us (0.957)
  waiting for transfers between devices: 241 us -> 171 us
  blocking collectives: 37 us -> 81.3 us
  local copies, waits for them, and re-layouts: 54 us -> 67.7 us
  starting transfers between devices: 100 us -> 91.8 us
    all_to_all x2 -> x1, waiting for transfers between devices: 45.9 us -> 0.01 us  [body(): lax.all_to_all(jnp.stack([behind, forward], axis=1), 'slab', split_axis=2...]
    ppermute x16, waiting for transfers between devices: 183 us -> 149 us  [from_behind(): lax.ppermute(value, axis, [(i, (i + by) % peers) for i in range(peers)])]
    all_to_all x1, blocking collectives: 31.6 us -> 56.5 us  [body(): lax.all_to_all(as_sent(jnp.stack([retarded_local, lesser_local])[:, None]...]
    all_gather x1, blocking collectives: 5.31 us -> 24.9 us  [body(): level_whole = lax.all_gather(onsite, 'slab', axis=1, tiled=True)]
    all_to_all x3, waiting for transfers between devices: 11.4 us -> 20.9 us  [body(): lax.all_to_all(piece, 'slab', split_axis=1, concat_axis=2, tiled=True)]
    unnamed x105 -> x123, local copies, waits for them, and re-layouts: 39.1 us -> 45.3 us
    another operation x4 -> x8, other arithmetic: 0.47 us -> 6.18 us  [the longest x3 4.57 us: body(): jnp.stack([behind, forward], axis=1)]
  transfers between devices with their start and end apart: 23 -> 22, of which waited for: 16 -> 12; matrix products, arithmetic and copies ran while one was open for 10% -> 10% of each run, Pallas kernels for 0% -> 0%
where the time goes in v3:
time: 507 us; the launch traced here: 499 us
  waiting for transfers between devices  171 us (34%)
  starting transfers between devices  91.8 us (18%)
  blocking collectives  81.3 us (16%)
  local copies, waits for them, and re-layouts  67.7 us (13%)
  other arithmetic  41.5 us (8%)
  matrix products  28.1 us (6%)
  between operations  17.4 us (3%)
    ppermute x16, waiting for transfers between devices, from_behind(): lax.ppermute(value, axis, [(i, (i + by) % peers) for i in range(peers)])  149 us
    ppermute x16, starting transfers between devices, from_behind(): lax.ppermute(value, axis, [(i, (i + by) % peers) for i in range(peers)])  75 us
    all_to_all x1, blocking collectives, body(): lax.all_to_all(as_sent(jnp.stack([retarded_local, lesser_local])[:, None]...  56.5 us
    unnamed x123, local copies, waits for them, and re-layouts  45.3 us
    all_gather x1, blocking collectives, body(): level_whole = lax.all_gather(onsite, 'slab', axis=1, tiled=True)  24.9 us
    all_to_all x3, waiting for transfers between devices, body(): lax.all_to_all(piece, 'slab', split_axis=1, concat_axis=2, tiled=True)  20.9 us
    add x4, other arithmetic, weigh(): strength[0] * behind.astype(jnp.float32)  13.9 us
    all_to_all x3, starting transfers between devices, body(): lax.all_to_all(piece, 'slab', split_axis=1, concat_axis=2, tiled=True)  12.3 us
  transfers between devices with their start and end apart: 22, of which 12 were waited for; matrix products, arithmetic and copies ran while one was open for 10% of the time, Pallas kernels for 0%

profile of v3, /device:TPU:12, one launch (start us, length us, event | category | flops | bytes accessed | tf_op | source)
XLA Modules:
  0.0 498.6 jit_solution(15789272200774401193)
XLA Ops:
  7.9 4.0 fusion.324
  16.2 4.3 all-to-all-start.3
  25.0 20.9 %all-to-all-done.3 = bf16[1,4,1,1,1,384,384]{5,6,4,3,2,0,1:T(8,128)(2,1)} async-done(((bf16[1,4,1,1,1,384,384]{5,6,4,3,2,0,1:T(8,128)(2,1)}), bf16[1,4,1,1,1,384,384]{5,6,4,3,2,0,1:T(8,128)(2,1)}, u32[]{:S(2)}, u32[]{:S(2)}) %all-to-all-start.3) | async-done | bytes 1179680 | tf_op jit(solution)/shard_map/all_to_all | solution.py:175
  48.5 4.4 all-to-all-start.2
  53.8 17.4 %collective-permute-start.12 = (bf16[1,1,4,1,1,384,384]{5,6,2,4,3,1,0:T(8,128)(2,1)}, bf16[1,1,4,1,1,384,384]{5,6,2,4,3,1,0:T(8,128)(2,1)}, u32[]{:S(2)}, u32[]{:S(2)}) collective-permute-start(bf16[1,1,4,1,1,384,384]{5,6,2,4,3,1,0:T(8,128)(2,1)} %bitcast.53), channel_id=1, source_target_pairs={{0,1},{1,2},{2,3},{3,4},{4,5},{5,6},{6,7},{7,0},{8,9},{9,10},{10,1... | collective-permute-start | bytes 3538952 | tf_op jit(solution)/shard_map/ppermute | solution.py:13
  75.2 3.6 all-to-all-start.1
  82.1 20.2 %collective-permute-done.1 = bf16[1,4,1,1,1,384,384]{5,6,1,4,3,2,0:T(8,128)(2,1)} collective-permute-done((bf16[1,4,1,1,1,384,384]{5,6,1,4,3,2,0:T(8,128)(2,1)}, bf16[1,4,1,1,1,384,384]{5,6,1,4,3,2,0:T(8,128)(2,1)}, u32[]{:S(2)}, u32[]{:S(2)}) %collective-permute-start.1) | collective-permute-done | bytes 1179680 | tf_op jit(solution)/shard_map/ppermute | solution.py:13
  102.4 17.9 %collective-permute-done.14 = bf16[1,1,4,1,1,384,384]{5,6,2,4,3,1,0:T(8,128)(2,1)} collective-permute-done((bf16[1,1,4,1,1,384,384]{5,6,2,4,3,1,0:T(8,128)(2,1)}, bf16[1,1,4,1,1,384,384]{5,6,2,4,3,1,0:T(8,128)(2,1)}, u32[]{:S(2)}, u32[]{:S(2)}) %collective-permute-start.14) | collective-permute-done | bytes 1179680 | tf_op jit(solution)/shard_map/ppermute | solution.py:13
  120.7 5.5 %collective-permute-done.15 = bf16[1,1,4,1,1,384,384]{5,6,2,4,3,1,0:T(8,128)(2,1)} collective-permute-done((bf16[1,1,4,1,1,384,384]{5,6,2,4,3,1,0:T(8,128)(2,1)}, bf16[1,1,4,1,1,384,384]{5,6,2,4,3,1,0:T(8,128)(2,1)}, u32[]{:S(2)}, u32[]{:S(2)}) %collective-permute-start.15) | collective-permute-done | bytes 1179680 | tf_op jit(solution)/shard_map/ppermute | solution.py:13
  126.1 21.0 %collective-permute-start.8 = (bf16[1,1,4,1,1,384,384]{5,6,2,4,3,1,0:T(8,128)(2,1)}, bf16[1,1,4,1,1,384,384]{5,6,2,4,3,1,0:T(8,128)(2,1)}, u32[]{:S(2)}, u32[]{:S(2)}) collective-permute-start(bf16[1,1,4,1,1,384,384]{5,6,2,4,3,1,0:T(8,128)(2,1)} %bitcast.50), channel_id=1, source_target_pairs={{0,1},{1,2},{2,3},{3,4},{4,5},{5,6},{6,7},{7,0},{8,9},{9,10},{10,1... | collective-permute-start | bytes 3538952 | tf_op jit(solution)/shard_map/ppermute | solution.py:13
  158.1 4.5 all-to-all-start
  167.2 24.9 %all_gather.9 = f32[1,4,384]{2,0,1:T(1,128)S(1)} all-gather(f32[1,1,384]{2,0,1:T(1,128)S(1)} %bitcast.990), channel_id=1, replica_groups=mesh['slab'=4,'kt'=8] {'slab'}, dimensions={1}, use_global_device_ids=true | all-gather | bytes 7680 | tf_op jit(solution)/shard_map/all_gather | solution.py:184
  196.6 5.4 %collective-permute-done.11 = bf16[1,1,4,1,1,384,384]{5,6,2,4,3,1,0:T(8,128)(2,1)} collective-permute-done((bf16[1,1,4,1,1,384,384]{5,6,2,4,3,1,0:T(8,128)(2,1)}, bf16[1,1,4,1,1,384,384]{5,6,2,4,3,1,0:T(8,128)(2,1)}, u32[]{:S(2)}, u32[]{:S(2)}) %collective-permute-start.11) | collective-permute-done | bytes 1179680 | tf_op jit(solution)/shard_map/ppermute | solution.py:13
  201.9 21.1 %collective-permute-start.4 = (bf16[1,1,4,1,1,384,384]{5,6,2,4,3,1,0:T(8,128)(2,1)}, bf16[1,1,4,1,1,384,384]{5,6,2,4,3,1,0:T(8,128)(2,1)S(1)}, u32[]{:S(2)}, u32[]{:S(2)}) collective-permute-start(bf16[1,1,4,1,1,384,384]{5,6,2,4,3,1,0:T(8,128)(2,1)} %bitcast.986), channel_id=1, source_target_pairs={{0,1},{1,2},{2,3},{3,4},{4,5},{5,6},{6,7},{7,0},{8,9},{9,10},{10,1... | collective-permute-start | bytes 3538952 | tf_op jit(solution)/shard_map/ppermute | solution.py:13
  223.1 4.1 collective-permute-done.8
  228.9 3.5 add_bitcast_fusion
  232.4 21.8 %collective-permute-done.9 = bf16[1,1,4,1,1,384,384]{5,6,2,4,3,1,0:T(8,128)(2,1)} collective-permute-done((bf16[1,1,4,1,1,384,384]{5,6,2,4,3,1,0:T(8,128)(2,1)}, bf16[1,1,4,1,1,384,384]{5,6,2,4,3,1,0:T(8,128)(2,1)}, u32[]{:S(2)}, u32[]{:S(2)}) %collective-permute-start.9) | collective-permute-done | bytes 1179680 | tf_op jit(solution)/shard_map/ppermute | solution.py:13
  254.2 4.9 add_bitcast_fusion.1
  259.1 12.7 %collective-permute-done.6 = bf16[1,1,4,1,1,384,384]{5,6,2,4,3,1,0:T(8,128)(2,1)S(1)} collective-permute-done((bf16[1,1,4,1,1,384,384]{5,6,2,4,3,1,0:T(8,128)(2,1)}, bf16[1,1,4,1,1,384,384]{5,6,2,4,3,1,0:T(8,128)(2,1)S(1)}, u32[]{:S(2)}, u32[]{:S(2)}) %collective-permute-start.6) | collective-permute-done | bytes 1179680 | tf_op jit(solution)/shard_map/ppermute | solution.py:13
  271.8 4.8 collective-permute-done.7
  276.5 26.5 %collective-permute-done.4 = bf16[1,1,4,1,1,384,384]{5,6,2,4,3,1,0:T(8,128)(2,1)S(1)} collective-permute-done((bf16[1,1,4,1,1,384,384]{5,6,2,4,3,1,0:T(8,128)(2,1)}, bf16[1,1,4,1,1,384,384]{5,6,2,4,3,1,0:T(8,128)(2,1)S(1)}, u32[]{:S(2)}, u32[]{:S(2)}) %collective-permute-start.4) | collective-permute-done | bytes 1179680 | tf_op jit(solution)/shard_map/ppermute | solution.py:13
  303.0 26.4 %collective-permute-done.5 = bf16[1,1,4,1,1,384,384]{5,6,2,4,3,1,0:T(8,128)(2,1)S(1)} collective-permute-done((bf16[1,1,4,1,1,384,384]{5,6,2,4,3,1,0:T(8,128)(2,1)}, bf16[1,1,4,1,1,384,384]{5,6,2,4,3,1,0:T(8,128)(2,1)S(1)}, u32[]{:S(2)}, u32[]{:S(2)}) %collective-permute-start.5) | collective-permute-done | bytes 1179680 | tf_op jit(solution)/shard_map/ppermute | solution.py:13
  426.1 56.5 %all_to_all.57 = bf16[2,1,1,4,2,384,384]{5,6,4,0,2,1,3:T(8,128)(2,1)S(1)} all-to-all(bf16[2,1,1,4,2,384,384]{5,6,4,0,2,1,3:T(8,128)(2,1)S(1)} %copy.292), channel_id=1, replica_groups=mesh['slab'=4,'kt'=8] {'slab'}, dimensions={3} | all-to-all | bytes 9437184 | tf_op jit(solution)/shard_map/all_to_all | solution.py:199
  484.5 4.3 copy.293
  (272 shorter events, 140.9 us)
Async XLA Ops:
  7.2 335.2 %all-gather.5.cloned.1.call-start = ((), (), s32[]{:S(2)}) async-start(), calls=%async_computation.6 | async-start | bytes 2949120 | tf_op jit(solution)/shard_map/all_gather | solution.py:187
  14.2 32.2 %collective-permute-start.2 = (bf16[1,4,1,1,1,384,384]{5,6,1,4,3,2,0:T(8,128)(2,1)}, bf16[1,4,1,1,1,384,384]{5,6,1,4,3,2,0:T(8,128)(2,1)}, u32[]{:S(2)}, u32[]{:S(2)}) collective-permute-start(bf16[1,4,1,1,1,384,384]{5,6,1,4,3,2,0:T(8,128)(2,1)} %copy.388), channel_id=1, source_target_pairs={{0,7},{1,0},{2,1},{3,2},{4,3},{5,4},{6,5},{7,6},{8,15},{9,8},{10,9... | collective-permute-start | bytes 3538952 | tf_op jit(solution)/shard_map/ppermute | solution.py:13
  16.2 29.7 %all-to-all-start.3 = ((bf16[1,4,1,1,1,384,384]{5,6,4,3,2,0,1:T(8,128)(2,1)}), bf16[1,4,1,1,1,384,384]{5,6,4,3,2,0,1:T(8,128)(2,1)}, u32[]{:S(2)}, u32[]{:S(2)}) async-start(bf16[1,4,1,1,1,384,384]{5,6,4,3,2,0,1:T(8,128)(2,1)} %copy.391), calls=%async_computation.3 | async-start | bytes 2359296 | tf_op jit(solution)/shard_map/all_to_all | solution.py:175
  20.5 33.3 %collective-permute-start.3 = (bf16[1,4,1,1,1,384,384]{5,6,1,4,3,2,0:T(8,128)(2,1)}, bf16[1,4,1,1,1,384,384]{5,6,1,4,3,2,0:T(8,128)(2,1)}, u32[]{:S(2)}, u32[]{:S(2)}) collective-permute-start(bf16[1,4,1,1,1,384,384]{5,6,1,4,3,2,0:T(8,128)(2,1)} %copy.388), channel_id=1, source_target_pairs={{0,6},{1,7},{2,0},{3,1},{4,2},{5,3},{6,4},{7,5},{8,14},{9,15},{10,... | collective-permute-start | bytes 3538952 | tf_op jit(solution)/shard_map/ppermute | solution.py:13
  20.6 58.2 %collective-permute-start = (bf16[1,4,1,1,1,384,384]{5,6,1,4,3,2,0:T(8,128)(2,1)}, bf16[1,4,1,1,1,384,384]{5,6,1,4,3,2,0:T(8,128)(2,1)}, u32[]{:S(2)}, u32[]{:S(2)}) collective-permute-start(bf16[1,4,1,1,1,384,384]{5,6,1,4,3,2,0:T(8,128)(2,1)} %copy.388), channel_id=1, source_target_pairs={{0,1},{1,2},{2,3},{3,4},{4,5},{5,6},{6,7},{7,0},{8,9},{9,10},{10,1... | collective-permute-start | bytes 3538952 | tf_op jit(solution)/shard_map/ppermute | solution.py:13
  23.4 78.9 %collective-permute-start.1 = (bf16[1,4,1,1,1,384,384]{5,6,1,4,3,2,0:T(8,128)(2,1)}, bf16[1,4,1,1,1,384,384]{5,6,1,4,3,2,0:T(8,128)(2,1)}, u32[]{:S(2)}, u32[]{:S(2)}) collective-permute-start(bf16[1,4,1,1,1,384,384]{5,6,1,4,3,2,0:T(8,128)(2,1)} %copy.388), channel_id=1, source_target_pairs={{0,2},{1,3},{2,4},{3,5},{4,6},{5,7},{6,0},{7,1},{8,10},{9,11},{10,... | collective-permute-start | bytes 3538952 | tf_op jit(solution)/shard_map/ppermute | solution.py:13
  45.9 74.3 %collective-permute-start.14 = (bf16[1,1,4,1,1,384,384]{5,6,2,4,3,1,0:T(8,128)(2,1)}, bf16[1,1,4,1,1,384,384]{5,6,2,4,3,1,0:T(8,128)(2,1)}, u32[]{:S(2)}, u32[]{:S(2)}) collective-permute-start(bf16[1,1,4,1,1,384,384]{5,6,2,4,3,1,0:T(8,128)(2,1)} %bitcast.53), channel_id=1, source_target_pairs={{0,7},{1,0},{2,1},{3,2},{4,3},{5,4},{6,5},{7,6},{8,15},{9,8},{10,9... | collective-permute-start | bytes 3538952 | tf_op jit(solution)/shard_map/ppermute | solution.py:13
  46.5 79.7 %collective-permute-start.15 = (bf16[1,1,4,1,1,384,384]{5,6,2,4,3,1,0:T(8,128)(2,1)}, bf16[1,1,4,1,1,384,384]{5,6,2,4,3,1,0:T(8,128)(2,1)}, u32[]{:S(2)}, u32[]{:S(2)}) collective-permute-start(bf16[1,1,4,1,1,384,384]{5,6,2,4,3,1,0:T(8,128)(2,1)} %bitcast.53), channel_id=1, source_target_pairs={{0,6},{1,7},{2,0},{3,1},{4,2},{5,3},{6,4},{7,5},{8,14},{9,15},{10,... | collective-permute-start | bytes 3538952 | tf_op jit(solution)/shard_map/ppermute | solution.py:13
  48.5 26.7 %all-to-all-start.2 = ((bf16[1,4,1,1,1,384,384]{5,6,4,3,2,0,1:T(8,128)(2,1)}), bf16[1,4,1,1,1,384,384]{5,6,4,3,2,0,1:T(8,128)(2,1)}, u32[]{:S(2)}, u32[]{:S(2)}) async-start(bf16[1,4,1,1,1,384,384]{5,6,4,3,2,0,1:T(8,128)(2,1)} %copy.390), calls=%async_computation.2 | async-start | bytes 2359296 | tf_op jit(solution)/shard_map/all_to_all | solution.py:175
  52.9 296.0 %all-gather.3.cloned.1.call-start = ((), (), s32[]{:S(2)}) async-start(), calls=%async_computation.5 | async-start | bytes 2949120 | tf_op jit(solution)/shard_map/all_gather | solution.py:186
  53.8 98.2 %collective-permute-start.12 = (bf16[1,1,4,1,1,384,384]{5,6,2,4,3,1,0:T(8,128)(2,1)}, bf16[1,1,4,1,1,384,384]{5,6,2,4,3,1,0:T(8,128)(2,1)}, u32[]{:S(2)}, u32[]{:S(2)}) collective-permute-start(bf16[1,1,4,1,1,384,384]{5,6,2,4,3,1,0:T(8,128)(2,1)} %bitcast.53), channel_id=1, source_target_pairs={{0,1},{1,2},{2,3},{3,4},{4,5},{5,6},{6,7},{7,0},{8,9},{9,10},{10,1... | collective-permute-start | bytes 3538952 | tf_op jit(solution)/shard_map/ppermute | solution.py:13
  75.1 73.7 %copy-start.51 = (f32[4]{0:T(128)S(1)}, f32[4]{0:T(128)}, u32[]{:S(2)}) copy-start(f32[4]{0:T(128)} %param.17) | copy-start | bytes 52
  75.2 73.7 %copy-start.52 = (s32[1,2]{1,0:T(1,128)S(1)}, s32[1,2]{1,0:T(1,128)}, u32[]{:S(2)}) copy-start(s32[1,2]{1,0:T(1,128)} %param.16) | copy-start | bytes 28
  75.2 81.9 %all-to-all-start.1 = ((bf16[1,4,1,1,1,384,384]{5,6,4,3,2,0,1:T(8,128)(2,1)}), bf16[1,4,1,1,1,384,384]{5,6,4,3,2,0,1:T(8,128)(2,1)S(1)}, u32[]{:S(2)}, u32[]{:S(2)}) async-start(bf16[1,4,1,1,1,384,384]{5,6,4,3,2,0,1:T(8,128)(2,1)} %copy.389), calls=%async_computation.1 | async-start | bytes 2359296 | tf_op jit(solution)/shard_map/all_to_all | solution.py:175
  78.7 113.9 %collective-permute-start.13 = (bf16[1,1,4,1,1,384,384]{5,6,2,4,3,1,0:T(8,128)(2,1)}, bf16[1,1,4,1,1,384,384]{5,6,2,4,3,1,0:T(8,128)(2,1)}, u32[]{:S(2)}, u32[]{:S(2)}) collective-permute-start(bf16[1,1,4,1,1,384,384]{5,6,2,4,3,1,0:T(8,128)(2,1)} %bitcast.53), channel_id=1, source_target_pairs={{0,2},{1,3},{2,4},{3,5},{4,6},{5,7},{6,0},{7,1},{8,10},{9,11},{10,... | collective-permute-start | bytes 3538952 | tf_op jit(solution)/shard_map/ppermute | solution.py:13
  102.3 93.7 %collective-permute-start.10 = (bf16[1,1,4,1,1,384,384]{5,6,2,4,3,1,0:T(8,128)(2,1)}, bf16[1,1,4,1,1,384,384]{5,6,2,4,3,1,0:T(8,128)(2,1)}, u32[]{:S(2)}, u32[]{:S(2)}) collective-permute-start(bf16[1,1,4,1,1,384,384]{5,6,2,4,3,1,0:T(8,128)(2,1)} %bitcast.50), channel_id=1, source_target_pairs={{0,7},{1,0},{2,1},{3,2},{4,3},{5,4},{6,5},{7,6},{8,15},{9,8},{10,9... | collective-permute-start | bytes 3538952 | tf_op jit(solution)/shard_map/ppermute | solution.py:13
  120.2 81.7 %collective-permute-start.11 = (bf16[1,1,4,1,1,384,384]{5,6,2,4,3,1,0:T(8,128)(2,1)}, bf16[1,1,4,1,1,384,384]{5,6,2,4,3,1,0:T(8,128)(2,1)}, u32[]{:S(2)}, u32[]{:S(2)}) collective-permute-start(bf16[1,1,4,1,1,384,384]{5,6,2,4,3,1,0:T(8,128)(2,1)} %bitcast.50), channel_id=1, source_target_pairs={{0,6},{1,7},{2,0},{3,1},{4,2},{5,3},{6,4},{7,5},{8,14},{9,15},{10,... | collective-permute-start | bytes 3538952 | tf_op jit(solution)/shard_map/ppermute | solution.py:13
  126.1 101.0 %collective-permute-start.8 = (bf16[1,1,4,1,1,384,384]{5,6,2,4,3,1,0:T(8,128)(2,1)}, bf16[1,1,4,1,1,384,384]{5,6,2,4,3,1,0:T(8,128)(2,1)}, u32[]{:S(2)}, u32[]{:S(2)}) collective-permute-start(bf16[1,1,4,1,1,384,384]{5,6,2,4,3,1,0:T(8,128)(2,1)} %bitcast.50), channel_id=1, source_target_pairs={{0,1},{1,2},{2,3},{3,4},{4,5},{5,6},{6,7},{7,0},{8,9},{9,10},{10,1... | collective-permute-start | bytes 3538952 | tf_op jit(solution)/shard_map/ppermute | solution.py:13
  151.9 102.3 %collective-permute-start.9 = (bf16[1,1,4,1,1,384,384]{5,6,2,4,3,1,0:T(8,128)(2,1)}, bf16[1,1,4,1,1,384,384]{5,6,2,4,3,1,0:T(8,128)(2,1)}, u32[]{:S(2)}, u32[]{:S(2)}) collective-permute-start(bf16[1,1,4,1,1,384,384]{5,6,2,4,3,1,0:T(8,128)(2,1)} %bitcast.50), channel_id=1, source_target_pairs={{0,2},{1,3},{2,4},{3,5},{4,6},{5,7},{6,0},{7,1},{8,10},{9,11},{10,... | collective-permute-start | bytes 3538952 | tf_op jit(solution)/shard_map/ppermute | solution.py:13
  158.1 174.6 %all-to-all-start = ((bf16[1,2,4,1,1,1,384,384]{6,7,1,5,4,3,0,2:T(8,128)(2,1)}), bf16[1,2,4,1,1,1,384,384]{6,7,1,5,4,3,0,2:T(8,128)(2,1)}, u32[]{:S(2)}, u32[]{:S(2)}) async-start(bf16[1,2,4,1,1,1,384,384]{6,7,1,5,4,3,0,2:T(8,128)(2,1)} %pad_maximum_fusion.1), calls=%async_computation | async-start | bytes 4718592 | tf_op jit(solution)/shard_map/all_to_all | solution.py:166
  192.6 79.2 %collective-permute-start.6 = (bf16[1,1,4,1,1,384,384]{5,6,2,4,3,1,0:T(8,128)(2,1)}, bf16[1,1,4,1,1,384,384]{5,6,2,4,3,1,0:T(8,128)(2,1)S(1)}, u32[]{:S(2)}, u32[]{:S(2)}) collective-permute-start(bf16[1,1,4,1,1,384,384]{5,6,2,4,3,1,0:T(8,128)(2,1)} %bitcast.984), channel_id=1, source_target_pairs={{0,7},{1,0},{2,1},{3,2},{4,3},{5,4},{6,5},{7,6},{8,15},{9,8},{10,9... | collective-permute-start | bytes 3538952 | tf_op jit(solution)/shard_map/ppermute | solution.py:13
  196.1 80.5 %collective-permute-start.7 = (bf16[1,1,4,1,1,384,384]{5,6,2,4,3,1,0:T(8,128)(2,1)}, bf16[1,1,4,1,1,384,384]{5,6,2,4,3,1,0:T(8,128)(2,1)S(1)}, u32[]{:S(2)}, u32[]{:S(2)}) collective-permute-start(bf16[1,1,4,1,1,384,384]{5,6,2,4,3,1,0:T(8,128)(2,1)} %bitcast.985), channel_id=1, source_target_pairs={{0,6},{1,7},{2,0},{3,1},{4,2},{5,3},{6,4},{7,5},{8,14},{9,15},{10,... | collective-permute-start | bytes 3538952 | tf_op jit(solution)/shard_map/ppermute | solution.py:13
  201.9 101.1 %collective-permute-start.4 = (bf16[1,1,4,1,1,384,384]{5,6,2,4,3,1,0:T(8,128)(2,1)}, bf16[1,1,4,1,1,384,384]{5,6,2,4,3,1,0:T(8,128)(2,1)S(1)}, u32[]{:S(2)}, u32[]{:S(2)}) collective-permute-start(bf16[1,1,4,1,1,384,384]{5,6,2,4,3,1,0:T(8,128)(2,1)} %bitcast.986), channel_id=1, source_target_pairs={{0,1},{1,2},{2,3},{3,4},{4,5},{5,6},{6,7},{7,0},{8,9},{9,10},{10,1... | collective-permute-start | bytes 3538952 | tf_op jit(solution)/shard_map/ppermute | solution.py:13
  227.2 102.3 %collective-permute-start.5 = (bf16[1,1,4,1,1,384,384]{5,6,2,4,3,1,0:T(8,128)(2,1)}, bf16[1,1,4,1,1,384,384]{5,6,2,4,3,1,0:T(8,128)(2,1)S(1)}, u32[]{:S(2)}, u32[]{:S(2)}) collective-permute-start(bf16[1,1,4,1,1,384,384]{5,6,2,4,3,1,0:T(8,128)(2,1)} %bitcast.987), channel_id=1, source_target_pairs={{0,2},{1,3},{2,4},{3,5},{4,6},{5,7},{6,0},{7,1},{8,10},{9,11},{10,... | collective-permute-start | bytes 3538952 | tf_op jit(solution)/shard_map/ppermute | solution.py:13
  (52 other events, 236.1 us)
Sparse Core Ops, SparseCore 0:
  9.5 34.7 all-gather.4
  55.3 27.5 all-gather.2

commit v4 on v1

--- a/solution.py
+++ b/solution.py
@@ -128,9 +128,11 @@
         jnp.where(mode_index[0][:, None] == mode_table[None, :], mode_strength[None, :], 0.0),
         axis=1,
     )
-    return strength[0] * behind[0].astype(jnp.float32) + strength[1] * forward[0].astype(
-        jnp.float32
-    )
+    return strength, behind, forward
+
+
+def weigh(strength, behind, forward):
+    return strength[0] * behind.astype(jnp.float32) + strength[1] * forward.astype(jnp.float32)
 
 
 def starting_blocks(contact, energy_list):
@@ -152,14 +154,34 @@
     energies, onsite, hamiltonian, hopping, contact, previous, neighbours, mode_index, mode_strength
 ):
     position = lax.axis_index("slab")
-    regrouped = lax.all_to_all(previous, "slab", split_axis=1, concat_axis=2, tiled=True)
-    phonon_all = cycle_phonon(regrouped, neighbours, mode_index, mode_strength)
+    half = previous.shape[5] // 2
+    halves = [
+        lax.all_to_all(
+            previous[:, :, :, :, :, h * half : (h + 1) * half],
+            "slab",
+            split_axis=1,
+            concat_axis=2,
+            tiled=True,
+        )
+        for h in range(2)
+    ]
+    slab_total = halves[0].shape[2]
+    slab_list = [None] * slab_total
+    for slab_num in reversed(range(slab_total)):
+        row_list = []
+        for regrouped in halves:
+            strength, behind, forward = cycle_phonon(
+                regrouped[:, :, slab_num : slab_num + 1], neighbours, mode_index, mode_strength
+            )
+            row_list.append(weigh(strength, behind[0], forward[0]))
+        slab_list[slab_num] = jnp.concatenate(row_list, axis=4)
+    phonon_all = jnp.concatenate(slab_list, axis=1)
     level_whole = lax.all_gather(onsite, "slab", axis=1, tiled=True)
     hamilton_whole, coupling_whole = (
         lax.all_gather(hamiltonian, "slab", axis=1, tiled=True),
         lax.all_gather(hopping, "slab", axis=1, tiled=True),
     )
-    local_count = regrouped.shape[1]
+    local_count = phonon_all.shape[0]
     local_energies = lax.dynamic_slice_in_dim(energies, position * local_count, local_count, 0)
     initial = starting_blocks(contact, local_energies)
 
@@ -169,15 +191,14 @@
         )
 
     retarded_local, lesser_local, unused = jax.vmap(run_whole)(initial, local_energies, phonon_all)
-    retarded_all, lesser_all = (
-        lax.all_to_all(
-            as_sent(retarded_local[None]), "slab", split_axis=2, concat_axis=1, tiled=True
-        ),
-        lax.all_to_all(
-            as_sent(lesser_local[None]), "slab", split_axis=2, concat_axis=1, tiled=True
-        ),
-    )
-    return (retarded_all, lesser_all)
+    both_all = lax.all_to_all(
+        as_sent(jnp.stack([retarded_local, lesser_local])[:, None]),
+        "slab",
+        split_axis=3,
+        concat_axis=2,
+        tiled=True,
+    )
+    return (both_all[0], both_all[1])
 
 
 def solution(mesh):

time: 542 us -> 560 us (1.033); the launches traced: 539 us -> 550 us
  waiting for transfers between devices: 404 us -> 211 us
  local copies, waits for them, and re-layouts: 38.3 us -> 120 us
  blocking collectives: 5.36 us -> 61.7 us
  starting transfers between devices: 20 us -> 62.1 us
  other arithmetic: 28.2 us -> 49 us
    ppermute x4 -> x32, waiting for transfers between devices: 274 us -> 152 us  [from_behind(): lax.ppermute(value, axis, [(i, (i + by) % peers) for i in range(peers)])]
    all_to_all x3 -> x2, waiting for transfers between devices: 128 us -> 58.5 us  [body(): lax.all_to_all(previous[:, :, :, :, :, h * half:(h + 1) * half], 'slab',...]
    ppermute x0 -> x32, local copies, waits for them, and re-layouts: none -> 59.5 us  [from_behind(): lax.ppermute(value, axis, [(i, (i + by) % peers) for i in range(peers)])]
    all_to_all x0 -> x1, blocking collectives: none -> 56.5 us  [body(): lax.all_to_all(as_sent(jnp.stack([retarded_local, lesser_local])[:, None]...]
    ppermute x4 -> x32, starting transfers between devices: 6.75 us -> 54.2 us  [from_behind(): lax.ppermute(value, axis, [(i, (i + by) % peers) for i in range(peers)])]
    unnamed x50 -> x209, local copies, waits for them, and re-layouts: 27.4 us -> 42.5 us
    slice x2 -> x4, local copies, waits for them, and re-layouts: 0.76 us -> 10.3 us  [the longest x1 5.24 us: body(): previous[:, :, :, :, :, h * half:(h + 1) * half]]
    add x1 -> x8, other arithmetic: 11.8 us -> 20.3 us  [weigh(): strength[0] * behind.astype(jnp.float32)]
  transfers between devices with their start and end apart: 9 -> 36, of which waited for: 7 -> 23; matrix products, arithmetic and copies ran while one was open for 6% -> 19% of each run, Pallas kernels for 0% -> 0%
where the time goes in v4:
time: 560 us; the launch traced here: 550 us
  waiting for transfers between devices  211 us (38%)
  local copies, waits for them, and re-layouts  120 us (21%)
  starting transfers between devices  62.1 us (11%)
  blocking collectives  61.7 us (11%)
  other arithmetic  49 us (9%)
  matrix products  28.7 us (5%)
  between operations  17.7 us (3%)
    ppermute x32, waiting for transfers between devices, from_behind(): lax.ppermute(value, axis, [(i, (i + by) % peers) for i in range(peers)])  152 us
    ppermute x32, local copies, waits for them, and re-layouts, from_behind(): lax.ppermute(value, axis, [(i, (i + by) % peers) for i in range(peers)])  59.5 us
    all_to_all x2, waiting for transfers between devices, body(): lax.all_to_all(previous[:, :, :, :, :, h * half:(h + 1) * half], 'slab',...  58.5 us
    all_to_all x1, blocking collectives, body(): lax.all_to_all(as_sent(jnp.stack([retarded_local, lesser_local])[:, None]...  56.5 us
    ppermute x32, starting transfers between devices, from_behind(): lax.ppermute(value, axis, [(i, (i + by) % peers) for i in range(peers)])  54.2 us
    unnamed x209, local copies, waits for them, and re-layouts  42.5 us
    add x8, other arithmetic, weigh(): strength[0] * behind.astype(jnp.float32)  20.3 us
    dot_general x8, matrix products, mul_adjoint(): jnp.einsum('...pij,qkj->...pqik', first_op, second_op, preferred_element_...  11.4 us
  transfers between devices with their start and end apart: 36, of which 23 were waited for; matrix products, arithmetic and copies ran while one was open for 19% of the time, Pallas kernels for 0%

profile of v4, /device:TPU:0, one launch (start us, length us, event | category | flops | bytes accessed | tf_op | source)
XLA Modules:
  0.0 550.3 jit_solution(13757800717214204489)
XLA Ops:
  7.2 5.2 fusion.324
  17.4 40.4 %all-to-all-done.1 = bf16[1,4,1,2,2,192,384]{6,5,4,3,2,0,1:T(8,128)(2,1)S(1)} async-done(((bf16[1,4,1,2,2,192,384]{6,5,4,3,2,0,1:T(8,128)(2,1)}), bf16[1,4,1,2,2,192,384]{6,5,4,3,2,0,1:T(8,128)(2,1)S(1)}, u32[]{:S(2)}, u32[]{:S(2)}) %all-to-all-start.1) | async-done | bytes 2359328 | tf_op jit(solution)/shard_map/all_to_all | solution.py:159
  65.8 5.4 collective-permute-start.6
  73.2 18.1 %all-to-all-done = bf16[1,4,1,2,2,192,384]{6,5,4,3,2,0,1:T(8,128)(2,1)S(1)} async-done(((bf16[1,4,1,2,2,192,384]{6,5,4,3,2,0,1:T(8,128)(2,1)}), bf16[1,4,1,2,2,192,384]{6,5,4,3,2,0,1:T(8,128)(2,1)S(1)}, u32[]{:S(2)}, u32[]{:S(2)}) %all-to-all-start) | async-done | bytes 2359328 | tf_op jit(solution)/shard_map/all_to_all | solution.py:159
  92.8 5.4 collective-permute-start.2
  100.9 10.6 %collective-permute-done.5 = bf16[1,1,1,2,2,192,384]{6,5,4,3,2,1,0:T(8,128)(2,1)} collective-permute-done((bf16[1,1,1,2,2,192,384]{6,5,4,3,2,1,0:T(8,128)(2,1)}, bf16[1,1,1,2,2,192,384]{6,5,4,3,2,1,0:T(8,128)(2,1)}, u32[]{:S(2)}, u32[]{:S(2)}) %collective-permute-start.5) | collective-permute-done | bytes 589856 | tf_op jit(solution)/shard_map/ppermute | solution.py:13
  115.4 7.8 %collective-permute-done.2 = bf16[1,1,1,2,2,192,384]{6,5,4,3,2,1,0:T(8,128)(2,1)S(1)} collective-permute-done((bf16[1,1,1,2,2,192,384]{6,5,4,3,2,1,0:T(8,128)(2,1)}, bf16[1,1,1,2,2,192,384]{6,5,4,3,2,1,0:T(8,128)(2,1)S(1)}, u32[]{:S(2)}, u32[]{:S(2)}) %collective-permute-start.2) | collective-permute-done | bytes 589856 | tf_op jit(solution)/shard_map/ppermute | solution.py:13
  123.7 12.5 %collective-permute-done.3 = bf16[1,1,1,2,2,192,384]{6,5,4,3,2,1,0:T(8,128)(2,1)S(1)} collective-permute-done((bf16[1,1,1,2,2,192,384]{6,5,4,3,2,1,0:T(8,128)(2,1)}, bf16[1,1,1,2,2,192,384]{6,5,4,3,2,1,0:T(8,128)(2,1)S(1)}, u32[]{:S(2)}, u32[]{:S(2)}) %collective-permute-start.3) | collective-permute-done | bytes 589856 | tf_op jit(solution)/shard_map/ppermute | solution.py:13
  138.9 10.5 %collective-permute-done.1 = bf16[1,1,1,2,2,192,384]{6,5,4,3,2,1,0:T(8,128)(2,1)S(1)} collective-permute-done((bf16[1,1,1,2,2,192,384]{6,5,4,3,2,1,0:T(8,128)(2,1)}, bf16[1,1,1,2,2,192,384]{6,5,4,3,2,1,0:T(8,128)(2,1)S(1)}, u32[]{:S(2)}, u32[]{:S(2)}) %collective-permute-start.1) | collective-permute-done | bytes 589856 | tf_op jit(solution)/shard_map/ppermute | solution.py:13
  153.2 7.8 %collective-permute-done.14 = bf16[1,1,1,2,2,192,384]{6,5,4,3,2,1,0:T(8,128)(2,1)S(1)} collective-permute-done((bf16[1,1,1,2,2,192,384]{6,5,4,3,2,1,0:T(8,128)(2,1)S(1)}, bf16[1,1,1,2,2,192,384]{6,5,4,3,2,1,0:T(8,128)(2,1)S(1)}, u32[]{:S(2)}, u32[]{:S(2)}) %collective-permute-start.14) | collective-permute-done | bytes 589856 | tf_op jit(solution)/shard_map/ppermute | solution.py:13
  161.6 12.7 %collective-permute-done.15 = bf16[1,1,1,2,2,192,384]{6,5,4,3,2,1,0:T(8,128)(2,1)} collective-permute-done((bf16[1,1,1,2,2,192,384]{6,5,4,3,2,1,0:T(8,128)(2,1)S(1)}, bf16[1,1,1,2,2,192,384]{6,5,4,3,2,1,0:T(8,128)(2,1)}, u32[]{:S(2)}, u32[]{:S(2)}) %collective-permute-start.15) | collective-permute-done | bytes 589856 | tf_op jit(solution)/shard_map/ppermute | solution.py:13
  176.9 10.6 %collective-permute-done.13 = bf16[1,1,1,2,2,192,384]{6,5,4,3,2,1,0:T(8,128)(2,1)} collective-permute-done((bf16[1,1,1,2,2,192,384]{6,5,4,3,2,1,0:T(8,128)(2,1)S(1)}, bf16[1,1,1,2,2,192,384]{6,5,4,3,2,1,0:T(8,128)(2,1)}, u32[]{:S(2)}, u32[]{:S(2)}) %collective-permute-start.13) | collective-permute-done | bytes 589856 | tf_op jit(solution)/shard_map/ppermute | solution.py:13
  196.7 5.2 all_gather.9
  202.7 9.5 %collective-permute-done.11 = bf16[1,1,1,2,2,192,384]{6,5,4,3,2,1,0:T(8,128)(2,1)} collective-permute-done((bf16[1,1,1,2,2,192,384]{6,5,4,3,2,1,0:T(8,128)(2,1)}, bf16[1,1,1,2,2,192,384]{6,5,4,3,2,1,0:T(8,128)(2,1)}, u32[]{:S(2)}, u32[]{:S(2)}) %collective-permute-start.11) | collective-permute-done | bytes 589856 | tf_op jit(solution)/shard_map/ppermute | solution.py:13
  214.9 10.6 %collective-permute-done.9 = bf16[1,1,1,2,2,192,384]{6,5,4,3,2,1,0:T(8,128)(2,1)} collective-permute-done((bf16[1,1,1,2,2,192,384]{6,5,4,3,2,1,0:T(8,128)(2,1)}, bf16[1,1,1,2,2,192,384]{6,5,4,3,2,1,0:T(8,128)(2,1)}, u32[]{:S(2)}, u32[]{:S(2)}) %collective-permute-start.9) | collective-permute-done | bytes 589856 | tf_op jit(solution)/shard_map/ppermute | solution.py:13
  229.2 7.9 %collective-permute-done.22 = bf16[1,1,1,2,2,192,384]{6,5,4,3,2,1,0:T(8,128)(2,1)} collective-permute-done((bf16[1,1,1,2,2,192,384]{6,5,4,3,2,1,0:T(8,128)(2,1)}, bf16[1,1,1,2,2,192,384]{6,5,4,3,2,1,0:T(8,128)(2,1)}, u32[]{:S(2)}, u32[]{:S(2)}) %collective-permute-start.22) | collective-permute-done | bytes 589856 | tf_op jit(solution)/shard_map/ppermute | solution.py:13
  259.9 5.2 collective-permute-start.16
  268.4 6.7 %collective-permute-done.18 = bf16[1,1,1,2,2,192,384]{6,5,4,3,2,1,0:T(8,128)(2,1)} collective-permute-done((bf16[1,1,1,2,2,192,384]{6,5,4,3,2,1,0:T(8,128)(2,1)}, bf16[1,1,1,2,2,192,384]{6,5,4,3,2,1,0:T(8,128)(2,1)}, u32[]{:S(2)}, u32[]{:S(2)}) %collective-permute-start.18) | collective-permute-done | bytes 589856 | tf_op jit(solution)/shard_map/ppermute | solution.py:13
  275.7 12.3 %collective-permute-done.19 = bf16[1,1,1,2,2,192,384]{6,5,4,3,2,1,0:T(8,128)(2,1)} collective-permute-done((bf16[1,1,1,2,2,192,384]{6,5,4,3,2,1,0:T(8,128)(2,1)}, bf16[1,1,1,2,2,192,384]{6,5,4,3,2,1,0:T(8,128)(2,1)}, u32[]{:S(2)}, u32[]{:S(2)}) %collective-permute-start.19) | collective-permute-done | bytes 589856 | tf_op jit(solution)/shard_map/ppermute | solution.py:13
  295.7 5.7 %collective-permute-done.17 = bf16[1,1,1,2,2,192,384]{6,5,4,3,2,1,0:T(8,128)(2,1)S(1)} collective-permute-done((bf16[1,1,1,2,2,192,384]{6,5,4,3,2,1,0:T(8,128)(2,1)}, bf16[1,1,1,2,2,192,384]{6,5,4,3,2,1,0:T(8,128)(2,1)S(1)}, u32[]{:S(2)}, u32[]{:S(2)}) %collective-permute-start.17) | collective-permute-done | bytes 589856 | tf_op jit(solution)/shard_map/ppermute | solution.py:13
  304.9 8.2 %collective-permute-done.30 = bf16[1,1,1,2,2,192,384]{6,5,4,3,2,1,0:T(8,128)(2,1)S(1)} collective-permute-done((bf16[1,1,1,2,2,192,384]{6,5,4,3,2,1,0:T(8,128)(2,1)}, bf16[1,1,1,2,2,192,384]{6,5,4,3,2,1,0:T(8,128)(2,1)S(1)}, u32[]{:S(2)}, u32[]{:S(2)}) %collective-permute-start.30) | collective-permute-done | bytes 589856 | tf_op jit(solution)/shard_map/ppermute | solution.py:13
  313.7 12.1 %collective-permute-done.31 = bf16[1,1,1,2,2,192,384]{6,5,4,3,2,1,0:T(8,128)(2,1)S(1)} collective-permute-done((bf16[1,1,1,2,2,192,384]{6,5,4,3,2,1,0:T(8,128)(2,1)}, bf16[1,1,1,2,2,192,384]{6,5,4,3,2,1,0:T(8,128)(2,1)S(1)}, u32[]{:S(2)}, u32[]{:S(2)}) %collective-permute-start.31) | collective-permute-done | bytes 589856 | tf_op jit(solution)/shard_map/ppermute | solution.py:13
  340.0 4.4 add_bitcast_fusion.5
  477.8 56.5 %all_to_all.33 = bf16[2,1,1,4,2,384,384]{5,6,4,0,2,1,3:T(8,128)(2,1)S(1)} all-to-all(bf16[2,1,1,4,2,384,384]{5,6,4,0,2,1,3:T(8,128)(2,1)S(1)} %copy.339), channel_id=1, replica_groups=mesh['slab'=4,'kt'=8] {'slab'}, dimensions={3} | all-to-all | bytes 9437184 | tf_op jit(solution)/shard_map/all_to_all | solution.py:194
  (421 shorter events, 241.4 us)
Async XLA Ops:
  12.4 45.4 %all-to-all-start.1 = ((bf16[1,4,1,2,2,192,384]{6,5,4,3,2,0,1:T(8,128)(2,1)}), bf16[1,4,1,2,2,192,384]{6,5,4,3,2,0,1:T(8,128)(2,1)S(1)}, u32[]{:S(2)}, u32[]{:S(2)}) async-start(bf16[1,4,1,2,2,192,384]{6,5,4,3,2,0,1:T(8,128)(2,1)} %get-tuple-element.57), calls=%async_computation.1 | async-start | bytes 4718592 | tf_op jit(solution)/shard_map/all_to_all | solution.py:159
  16.6 376.3 %all-gather.5.cloned.1.call-start = ((), (), s32[]{:S(2)}) async-start(), calls=%async_computation.4 | async-start | bytes 2949120 | tf_op jit(solution)/shard_map/all_gather | solution.py:182
  62.8 337.5 %all-gather.3.cloned.1.call-start = ((), (), s32[]{:S(2)}) async-start(), calls=%async_computation.3 | async-start | bytes 2949120 | tf_op jit(solution)/shard_map/all_gather | solution.py:181
  72.2 39.2 %collective-permute-start.5 = (bf16[1,1,1,2,2,192,384]{6,5,4,3,2,1,0:T(8,128)(2,1)}, bf16[1,1,1,2,2,192,384]{6,5,4,3,2,1,0:T(8,128)(2,1)}, u32[]{:S(2)}, u32[]{:S(2)}) collective-permute-start(bf16[1,1,1,2,2,192,384]{6,5,4,3,2,1,0:T(8,128)(2,1)} %get-tuple-element.77), channel_id=1, source_target_pairs={{0,2},{1,3},{2,4},{3,5},{4,6},{5,7},{6,0},{7,1},{8,10},{9,11},{10,... | collective-permute-start | bytes 1769480 | tf_op jit(solution)/shard_map/ppermute | solution.py:13
  99.3 50.0 %collective-permute-start.1 = (bf16[1,1,1,2,2,192,384]{6,5,4,3,2,1,0:T(8,128)(2,1)}, bf16[1,1,1,2,2,192,384]{6,5,4,3,2,1,0:T(8,128)(2,1)S(1)}, u32[]{:S(2)}, u32[]{:S(2)}) collective-permute-start(bf16[1,1,1,2,2,192,384]{6,5,4,3,2,1,0:T(8,128)(2,1)} %get-tuple-element.73), channel_id=1, source_target_pairs={{0,2},{1,3},{2,4},{3,5},{4,6},{5,7},{6,0},{7,1},{8,10},{9,11},{10,... | collective-permute-start | bytes 1769480 | tf_op jit(solution)/shard_map/ppermute | solution.py:13
  111.5 49.6 %collective-permute-start.14 = (bf16[1,1,1,2,2,192,384]{6,5,4,3,2,1,0:T(8,128)(2,1)S(1)}, bf16[1,1,1,2,2,192,384]{6,5,4,3,2,1,0:T(8,128)(2,1)S(1)}, u32[]{:S(2)}, u32[]{:S(2)}) collective-permute-start(bf16[1,1,1,2,2,192,384]{6,5,4,3,2,1,0:T(8,128)(2,1)S(1)} %get-tuple-element.76), channel_id=1, source_target_pairs={{0,7},{1,0},{2,1},{3,2},{4,3},{5,4},{6,5},{7,6},{8,15},{9,8},{10,9... | collective-permute-start | bytes 1769480 | tf_op jit(solution)/shard_map/ppermute | solution.py:13
  123.2 51.1 %collective-permute-start.15 = (bf16[1,1,1,2,2,192,384]{6,5,4,3,2,1,0:T(8,128)(2,1)S(1)}, bf16[1,1,1,2,2,192,384]{6,5,4,3,2,1,0:T(8,128)(2,1)}, u32[]{:S(2)}, u32[]{:S(2)}) collective-permute-start(bf16[1,1,1,2,2,192,384]{6,5,4,3,2,1,0:T(8,128)(2,1)S(1)} %get-tuple-element.76), channel_id=1, source_target_pairs={{0,6},{1,7},{2,0},{3,1},{4,2},{5,3},{6,4},{7,5},{8,14},{9,15},{10,... | collective-permute-start | bytes 1769480 | tf_op jit(solution)/shard_map/ppermute | solution.py:13
  137.2 50.3 %collective-permute-start.13 = (bf16[1,1,1,2,2,192,384]{6,5,4,3,2,1,0:T(8,128)(2,1)S(1)}, bf16[1,1,1,2,2,192,384]{6,5,4,3,2,1,0:T(8,128)(2,1)}, u32[]{:S(2)}, u32[]{:S(2)}) collective-permute-start(bf16[1,1,1,2,2,192,384]{6,5,4,3,2,1,0:T(8,128)(2,1)S(1)} %get-tuple-element.76), channel_id=1, source_target_pairs={{0,2},{1,3},{2,4},{3,5},{4,6},{5,7},{6,0},{7,1},{8,10},{9,11},{10,... | collective-permute-start | bytes 1769480 | tf_op jit(solution)/shard_map/ppermute | solution.py:13
  149.4 52.7 %collective-permute-start.10 = (bf16[1,1,1,2,2,192,384]{6,5,4,3,2,1,0:T(8,128)(2,1)}, bf16[1,1,1,2,2,192,384]{6,5,4,3,2,1,0:T(8,128)(2,1)}, u32[]{:S(2)}, u32[]{:S(2)}) collective-permute-start(bf16[1,1,1,2,2,192,384]{6,5,4,3,2,1,0:T(8,128)(2,1)} %get-tuple-element.72), channel_id=1, source_target_pairs={{0,7},{1,0},{2,1},{3,2},{4,3},{5,4},{6,5},{7,6},{8,15},{9,8},{10,9... | collective-permute-start | bytes 1769480 | tf_op jit(solution)/shard_map/ppermute | solution.py:13
  161.1 51.1 %collective-permute-start.11 = (bf16[1,1,1,2,2,192,384]{6,5,4,3,2,1,0:T(8,128)(2,1)}, bf16[1,1,1,2,2,192,384]{6,5,4,3,2,1,0:T(8,128)(2,1)}, u32[]{:S(2)}, u32[]{:S(2)}) collective-permute-start(bf16[1,1,1,2,2,192,384]{6,5,4,3,2,1,0:T(8,128)(2,1)} %get-tuple-element.72), channel_id=1, source_target_pairs={{0,6},{1,7},{2,0},{3,1},{4,2},{5,3},{6,4},{7,5},{8,14},{9,15},{10,... | collective-permute-start | bytes 1769480 | tf_op jit(solution)/shard_map/ppermute | solution.py:13
  175.3 50.2 %collective-permute-start.9 = (bf16[1,1,1,2,2,192,384]{6,5,4,3,2,1,0:T(8,128)(2,1)}, bf16[1,1,1,2,2,192,384]{6,5,4,3,2,1,0:T(8,128)(2,1)}, u32[]{:S(2)}, u32[]{:S(2)}) collective-permute-start(bf16[1,1,1,2,2,192,384]{6,5,4,3,2,1,0:T(8,128)(2,1)} %get-tuple-element.72), channel_id=1, source_target_pairs={{0,2},{1,3},{2,4},{3,5},{4,6},{5,7},{6,0},{7,1},{8,10},{9,11},{10,... | collective-permute-start | bytes 1769480 | tf_op jit(solution)/shard_map/ppermute | solution.py:13
  187.5 49.6 %collective-permute-start.22 = (bf16[1,1,1,2,2,192,384]{6,5,4,3,2,1,0:T(8,128)(2,1)}, bf16[1,1,1,2,2,192,384]{6,5,4,3,2,1,0:T(8,128)(2,1)}, u32[]{:S(2)}, u32[]{:S(2)}) collective-permute-start(bf16[1,1,1,2,2,192,384]{6,5,4,3,2,1,0:T(8,128)(2,1)} %get-tuple-element.75), channel_id=1, source_target_pairs={{0,7},{1,0},{2,1},{3,2},{4,3},{5,4},{6,5},{7,6},{8,15},{9,8},{10,9... | collective-permute-start | bytes 1769480 | tf_op jit(solution)/shard_map/ppermute | solution.py:13
  202.0 57.9 %collective-permute-start.23 = (bf16[1,1,1,2,2,192,384]{6,5,4,3,2,1,0:T(8,128)(2,1)}, bf16[1,1,1,2,2,192,384]{6,5,4,3,2,1,0:T(8,128)(2,1)}, u32[]{:S(2)}, u32[]{:S(2)}) collective-permute-start(bf16[1,1,1,2,2,192,384]{6,5,4,3,2,1,0:T(8,128)(2,1)} %get-tuple-element.75), channel_id=1, source_target_pairs={{0,6},{1,7},{2,0},{3,1},{4,2},{5,3},{6,4},{7,5},{8,14},{9,15},{10,... | collective-permute-start | bytes 1769480 | tf_op jit(solution)/shard_map/ppermute | solution.py:13
  212.2 53.0 %collective-permute-start.20 = (bf16[1,1,1,2,2,192,384]{6,5,4,3,2,1,0:T(8,128)(2,1)}, bf16[1,1,1,2,2,192,384]{6,5,4,3,2,1,0:T(8,128)(2,1)}, u32[]{:S(2)}, u32[]{:S(2)}) collective-permute-start(bf16[1,1,1,2,2,192,384]{6,5,4,3,2,1,0:T(8,128)(2,1)} %get-tuple-element.75), channel_id=1, source_target_pairs={{0,1},{1,2},{2,3},{3,4},{4,5},{5,6},{6,7},{7,0},{8,9},{9,10},{10,1... | collective-permute-start | bytes 1769480 | tf_op jit(solution)/shard_map/ppermute | solution.py:13
  213.2 51.9 %collective-permute-start.21 = (bf16[1,1,1,2,2,192,384]{6,5,4,3,2,1,0:T(8,128)(2,1)}, bf16[1,1,1,2,2,192,384]{6,5,4,3,2,1,0:T(8,128)(2,1)}, u32[]{:S(2)}, u32[]{:S(2)}) collective-permute-start(bf16[1,1,1,2,2,192,384]{6,5,4,3,2,1,0:T(8,128)(2,1)} %get-tuple-element.75), channel_id=1, source_target_pairs={{0,2},{1,3},{2,4},{3,5},{4,6},{5,7},{6,0},{7,1},{8,10},{9,11},{10,... | collective-permute-start | bytes 1769480 | tf_op jit(solution)/shard_map/ppermute | solution.py:13
  225.5 49.6 %collective-permute-start.18 = (bf16[1,1,1,2,2,192,384]{6,5,4,3,2,1,0:T(8,128)(2,1)}, bf16[1,1,1,2,2,192,384]{6,5,4,3,2,1,0:T(8,128)(2,1)}, u32[]{:S(2)}, u32[]{:S(2)}) collective-permute-start(bf16[1,1,1,2,2,192,384]{6,5,4,3,2,1,0:T(8,128)(2,1)} %get-tuple-element.71), channel_id=1, source_target_pairs={{0,7},{1,0},{2,1},{3,2},{4,3},{5,4},{6,5},{7,6},{8,15},{9,8},{10,9... | collective-permute-start | bytes 1769480 | tf_op jit(solution)/shard_map/ppermute | solution.py:13
  237.1 50.9 %collective-permute-start.19 = (bf16[1,1,1,2,2,192,384]{6,5,4,3,2,1,0:T(8,128)(2,1)}, bf16[1,1,1,2,2,192,384]{6,5,4,3,2,1,0:T(8,128)(2,1)}, u32[]{:S(2)}, u32[]{:S(2)}) collective-permute-start(bf16[1,1,1,2,2,192,384]{6,5,4,3,2,1,0:T(8,128)(2,1)} %get-tuple-element.71), channel_id=1, source_target_pairs={{0,6},{1,7},{2,0},{3,1},{4,2},{5,3},{6,4},{7,5},{8,14},{9,15},{10,... | collective-permute-start | bytes 1769480 | tf_op jit(solution)/shard_map/ppermute | solution.py:13
  265.1 47.9 %collective-permute-start.30 = (bf16[1,1,1,2,2,192,384]{6,5,4,3,2,1,0:T(8,128)(2,1)}, bf16[1,1,1,2,2,192,384]{6,5,4,3,2,1,0:T(8,128)(2,1)S(1)}, u32[]{:S(2)}, u32[]{:S(2)}) collective-permute-start(bf16[1,1,1,2,2,192,384]{6,5,4,3,2,1,0:T(8,128)(2,1)} %get-tuple-element.74), channel_id=1, source_target_pairs={{0,7},{1,0},{2,1},{3,2},{4,3},{5,4},{6,5},{7,6},{8,15},{9,8},{10,9... | collective-permute-start | bytes 1769480 | tf_op jit(solution)/shard_map/ppermute | solution.py:13
  275.1 50.7 %collective-permute-start.31 = (bf16[1,1,1,2,2,192,384]{6,5,4,3,2,1,0:T(8,128)(2,1)}, bf16[1,1,1,2,2,192,384]{6,5,4,3,2,1,0:T(8,128)(2,1)S(1)}, u32[]{:S(2)}, u32[]{:S(2)}) collective-permute-start(bf16[1,1,1,2,2,192,384]{6,5,4,3,2,1,0:T(8,128)(2,1)} %get-tuple-element.74), channel_id=1, source_target_pairs={{0,6},{1,7},{2,0},{3,1},{4,2},{5,3},{6,4},{7,5},{8,14},{9,15},{10,... | collective-permute-start | bytes 1769480 | tf_op jit(solution)/shard_map/ppermute | solution.py:13
  294.5 71.3 %collective-permute-start.29 = (bf16[1,1,1,2,2,192,384]{6,5,4,3,2,1,0:T(8,128)(2,1)}, bf16[1,1,1,2,2,192,384]{6,5,4,3,2,1,0:T(8,128)(2,1)}, u32[]{:S(2)}, u32[]{:S(2)}) collective-permute-start(bf16[1,1,1,2,2,192,384]{6,5,4,3,2,1,0:T(8,128)(2,1)} %get-tuple-element.74), channel_id=1, source_target_pairs={{0,2},{1,3},{2,4},{3,5},{4,6},{5,7},{6,0},{7,1},{8,10},{9,11},{10,... | collective-permute-start | bytes 1769480 | tf_op jit(solution)/shard_map/ppermute | solution.py:13
  301.4 66.7 %collective-permute-start.26 = (bf16[1,1,1,2,2,192,384]{6,5,4,3,2,1,0:T(8,128)(2,1)}, bf16[1,1,1,2,2,192,384]{6,5,4,3,2,1,0:T(8,128)(2,1)}, u32[]{:S(2)}, u32[]{:S(2)}) collective-permute-start(bf16[1,1,1,2,2,192,384]{6,5,4,3,2,1,0:T(8,128)(2,1)} %get-tuple-element.70), channel_id=1, source_target_pairs={{0,7},{1,0},{2,1},{3,2},{4,3},{5,4},{6,5},{7,6},{8,15},{9,8},{10,9... | collective-permute-start | bytes 1769480 | tf_op jit(solution)/shard_map/ppermute | solution.py:13
  313.1 57.2 %collective-permute-start.27 = (bf16[1,1,1,2,2,192,384]{6,5,4,3,2,1,0:T(8,128)(2,1)}, bf16[1,1,1,2,2,192,384]{6,5,4,3,2,1,0:T(8,128)(2,1)}, u32[]{:S(2)}, u32[]{:S(2)}) collective-permute-start(bf16[1,1,1,2,2,192,384]{6,5,4,3,2,1,0:T(8,128)(2,1)} %get-tuple-element.70), channel_id=1, source_target_pairs={{0,6},{1,7},{2,0},{3,1},{4,2},{5,3},{6,4},{7,5},{8,14},{9,15},{10,... | collective-permute-start | bytes 1769480 | tf_op jit(solution)/shard_map/ppermute | solution.py:13
  325.8 46.7 %collective-permute-start.24 = (bf16[1,1,1,2,2,192,384]{6,5,4,3,2,1,0:T(8,128)(2,1)}, bf16[1,1,1,2,2,192,384]{6,5,4,3,2,1,0:T(8,128)(2,1)}, u32[]{:S(2)}, u32[]{:S(2)}) collective-permute-start(bf16[1,1,1,2,2,192,384]{6,5,4,3,2,1,0:T(8,128)(2,1)} %get-tuple-element.70), channel_id=1, source_target_pairs={{0,1},{1,2},{2,3},{3,4},{4,5},{5,6},{6,7},{7,0},{8,9},{9,10},{10,1... | collective-permute-start | bytes 1769480 | tf_op jit(solution)/shard_map/ppermute | solution.py:13
  327.1 49.8 %collective-permute-start.25 = (bf16[1,1,1,2,2,192,384]{6,5,4,3,2,1,0:T(8,128)(2,1)}, bf16[1,1,1,2,2,192,384]{6,5,4,3,2,1,0:T(8,128)(2,1)}, u32[]{:S(2)}, u32[]{:S(2)}) collective-permute-start(bf16[1,1,1,2,2,192,384]{6,5,4,3,2,1,0:T(8,128)(2,1)} %get-tuple-element.70), channel_id=1, source_target_pairs={{0,2},{1,3},{2,4},{3,5},{4,6},{5,7},{6,0},{7,1},{8,10},{9,11},{10,... | collective-permute-start | bytes 1769480 | tf_op jit(solution)/shard_map/ppermute | solution.py:13
  (111 other events, 986.0 us)
Sparse Core Ops, SparseCore 0:
  19.0 39.4 all-gather.4
  138.9 24.6 all-gather.2
